TPU v7x, 32 devices: a whole 2x2x4 slice. The times are simulated.
32 devices in a mesh: brick: 8 (over y, x, core), tile: 4 (over z).
Axes of the slice: x: 2, y: 2, z: 4, core: 2. Of those that a mesh axis runs over, the one named last changes fastest.
Arguments:
- sample_grad: bfloat16 [28, 32768], P(None, ('brick', 'tile')), may hold values from -6 to 6
- sample_brick: int32 [32768], P(('brick', 'tile')), may hold values from 0 to 255, as said below
- sample_slot: int32 [32768], P(('brick', 'tile')), may hold values from 0 to 511
- neighbour: int32 [32, 6], P('brick'), may hold values from 0 to 31, as said below
Outputs:
- fine_grad: float32 [256, 28, 512], P(('brick', 'tile'))
- coarse_grad: float32 [32, 28, 512], P('brick', None, 'tile')
Inputs may be any that keep to these rules, and one draw needn't show every extreme that they name: `sample_brick`: of the 1024 samples of one device (consecutive along the samples), exactly 256 fall in the bricks of each of 4 owners (owner = brick // 32) and none in the others' bricks; some owners get 256 from every device. Of the 256 samples that one device has in one owner's bricks, exactly 64 lie in each group of 8 consecutive bricks of that owner. The relation is symmetric: neighbour[neighbour[b, k], k'] = b for the opposite face k'; no brick is its own neighbour. All face neighbours of a brick lie in its block of 4 consecutive coarse ids, the blocks starting at 2 and the last one wrapping around to id 0.
All inputs are finite; a program needn't handle non-finite values.
Results may differ from a plain program's by a relative error of at most 0.0003.
Values may be sent and summed in bfloat16 or wider, within the bound.
No kernel may reach another device: no remote copies, remote signals or barrier semaphores. Data moves between devices by JAX's collectives and lax.ppermute only.
A program may use at most 64 MiB of HBM per device.

v0:
```python
import jax
import jax.numpy as jnp
import numpy as np
from jax import lax
from jax.sharding import PartitionSpec as P

E = 8
V = 512
FACE = 64
CB_DEV = 4
FB_DEV = 32


row_block = 256


def extended_2(block, sides, width):
    for axis, dim in sides:
        count = lax.axis_size(axis)
        forward = [(i, i + 1) for i in range(count - 1)]
        forward.append((count - 1, 0))
        backward = [(target, source) for source, target in forward]
        low = lax.ppermute(
            lax.slice_in_dim(block, block.shape[dim] - width, None, axis=dim), axis, forward
        )
        high = lax.ppermute(lax.slice_in_dim(block, 0, width, axis=dim), axis, backward)
        block = jnp.concatenate([low, block, high], axis=dim)
    return block


def corners(fine_pos):
    is_even = fine_pos % 2 == 0
    lower_at = jnp.where(is_even, fine_pos // 2, fine_pos // 2 + 1)
    lower_w = jnp.where(is_even, 0.25, 0.75).astype(jnp.float32)
    return ((lower_at, lower_w), (lower_at + 1, 1.0 - lower_w))


def fold_column(pos_a, pos_b, pos_c, brick_edge):
    out_a = (pos_a == 0) | (pos_a == brick_edge + 1)
    out_b = (pos_b == 0) | (pos_b == brick_edge + 1)
    out_c = (pos_c == 0) | (pos_c == brick_edge + 1)
    outside = out_a.astype(jnp.int32) + out_b.astype(jnp.int32) + out_c.astype(jnp.int32)
    clamp_a = jnp.clip(pos_a, 1, brick_edge) - 1
    clamp_b = jnp.clip(pos_b, 1, brick_edge) - 1
    clamp_c = jnp.clip(pos_c, 1, brick_edge) - 1
    inner_col = clamp_a * brick_edge * brick_edge + clamp_b * brick_edge + clamp_c
    face_cells = brick_edge * brick_edge
    face_base = brick_edge**3
    face_a = (
        face_base
        + jnp.where(pos_a == 0, 0, 1) * face_cells
        + (pos_b - 1) * brick_edge
        + (pos_c - 1)
    )
    face_b = (
        face_base
        + (2 + jnp.where(pos_b == 0, 0, 1)) * face_cells
        + (pos_a - 1) * brick_edge
        + (pos_c - 1)
    )
    face_c = (
        face_base
        + (4 + jnp.where(pos_c == 0, 0, 1)) * face_cells
        + (pos_a - 1) * brick_edge
        + (pos_b - 1)
    )
    single = outside == 1
    return jnp.where(
        single & out_a,
        face_a,
        jnp.where(single & out_b, face_b, jnp.where(single & out_c, face_c, inner_col)),
    )


def child_matrix(child_id, row_count, brick_edge):
    slot_ids = jnp.arange(row_count, dtype=jnp.int32)
    coord_x = slot_ids // (brick_edge * brick_edge)
    coord_y = slot_ids // brick_edge % brick_edge
    coord_z = slot_ids % brick_edge
    fine_x = (child_id >> 2 & 1) * brick_edge + coord_x
    fine_y = (child_id >> 1 & 1) * brick_edge + coord_y
    fine_z = (child_id & 1) * brick_edge + coord_z
    column_total = brick_edge**3 + 6 * brick_edge * brick_edge
    column_ids = jnp.arange(column_total, dtype=jnp.int32)
    matrix = jnp.zeros((row_count, column_total), jnp.float32)
    for pos_a, weight_a in corners(fine_x):
        for pos_b, weight_b in corners(fine_y):
            for pos_c, weight_c in corners(fine_z):
                column = fold_column(pos_a, pos_b, pos_c, brick_edge)
                weight = weight_a * weight_b * weight_c
                matrix = matrix + jnp.where(
                    column[:, None] == column_ids[None, :], weight[:, None], 0.0
                )
    return matrix


def layer_matrix(brick_edge):
    grid_p, grid_q = np.meshgrid(np.arange(brick_edge), np.arange(brick_edge), indexing="ij")
    grid_p = grid_p.reshape(-1)
    grid_q = grid_q.reshape(-1)
    square = brick_edge * brick_edge
    last = brick_edge - 1
    layers = [
        grid_p * brick_edge + grid_q,
        last * square + grid_p * brick_edge + grid_q,
        grid_p * square + grid_q,
        grid_p * square + last * brick_edge + grid_q,
        grid_p * square + grid_q * brick_edge,
        grid_p * square + grid_q * brick_edge + last,
    ]
    cells = np.concatenate(layers)
    table = np.zeros((cells.shape[0], brick_edge**3), dtype=np.float32)
    table[np.arange(cells.shape[0]), cells] = 1.0
    return table


def rank_within(bucket_key):
    count = bucket_key.shape[0]
    order = jnp.arange(count, dtype=jnp.int32)
    earlier = (bucket_key[:, None] == bucket_key[None, :]) & (order[None, :] < order[:, None])
    return jnp.sum(earlier.astype(jnp.int32), axis=1)


def pack_rows(sample_grad, slot_code, bucket_at, slot_total):
    channels = sample_grad.shape[0]
    high_part = (slot_code // 128).astype(jnp.bfloat16)
    low_part = (slot_code % 128).astype(jnp.bfloat16)
    stacked = jnp.concatenate([sample_grad, high_part[None, :], low_part[None, :]], axis=0)
    hits = bucket_at[:, None] == jnp.arange(slot_total, dtype=jnp.int32)[None, :]
    placed = jnp.dot(stacked, hits.astype(jnp.bfloat16), preferred_element_type=jnp.float32)
    filled = jnp.any(hits, axis=0)
    high_row = jnp.where(filled, placed[channels], -1.0)
    moved = jnp.concatenate([placed[:channels], high_row[None, :], placed[channels + 1 :]], axis=0)
    return moved.astype(jnp.bfloat16)


def unpack_rows(arrived, channels):
    grad_rows = arrived[:channels]
    code_rows = arrived[channels].astype(jnp.int32) * 128 + arrived[channels + 1].astype(jnp.int32)
    return (grad_rows, code_rows)


def accumulate(grad_rows, code_rows, brick_count, slot_count):
    channels = grad_rows.shape[0]
    block_total = code_rows.shape[0] // row_block

    def add_block(block_id, running):
        start_row = block_id * row_block
        grad_part = lax.dynamic_slice_in_dim(grad_rows, start_row, row_block, 1)
        code_part = lax.dynamic_slice_in_dim(code_rows, start_row, row_block, 0)
        brick_part = jnp.where(code_part >= 0, code_part // slot_count, -1)
        slot_part = code_part % slot_count
        brick_hot = brick_part[None, :] == jnp.arange(brick_count, dtype=jnp.int32)[:, None]
        masked = jnp.where(brick_hot[:, None, :], grad_part[None, :, :], 0)
        slot_hot = (slot_part[:, None] == jnp.arange(slot_count, dtype=jnp.int32)[None, :]).astype(
            jnp.bfloat16
        )
        product = jnp.dot(
            masked.reshape(brick_count * channels, row_block),
            slot_hot,
            preferred_element_type=jnp.float32,
        )
        return running + product

    running = lax.fori_loop(
        0, block_total, add_block, jnp.zeros((brick_count * channels, slot_count), jnp.float32)
    )
    return running.reshape(brick_count, channels, slot_count)


def body(sample_grad, sample_brick, sample_slot, neighbour):
    tile_count = lax.axis_size("tile")
    owners = lax.axis_size("brick")
    tile_id = lax.axis_index("tile")
    brick_id = lax.axis_index("brick")
    samples = sample_brick.shape[0]
    channels = sample_grad.shape[0]
    capacity = 2 * samples // owners
    group_len = FB_DEV // tile_count
    group_cap = capacity // tile_count
    owner_of = sample_brick // FB_DEV
    local_brick = sample_brick - owner_of * FB_DEV
    group_of = local_brick // group_len
    bucket_key = owner_of * tile_count + group_of
    slot_code = (local_brick - group_of * group_len) * V + sample_slot
    bucket_at = bucket_key * group_cap + rank_within(bucket_key)
    packed = pack_rows(sample_grad, slot_code, bucket_at, owners * tile_count * group_cap)
    arrived = lax.all_to_all(
        lax.all_to_all(
            packed.reshape(channels + 2, owners, tile_count, group_cap),
            "brick",
            split_axis=1,
            concat_axis=1,
            tiled=True,
        ),
        "tile",
        split_axis=2,
        concat_axis=2,
        tiled=True,
    )
    grad_rows, code_rows = unpack_rows(
        arrived.reshape(channels + 2, owners * tile_count * group_cap), channels
    )
    fine_grad = accumulate(grad_rows, code_rows, group_len, V)
    family_count = max(group_len // 8, 1)
    first_fine = tile_id * group_len
    holder = jnp.zeros((family_count * 8, channels, V), jnp.float32)
    holder = lax.dynamic_update_slice_in_dim(holder, fine_grad, first_fine % (family_count * 8), 0)
    families = holder.reshape(family_count, 8, channels, V)
    part_padded = jnp.zeros((family_count, channels, V + 6 * FACE), jnp.float32)
    for child_id in range(8):
        matrix = child_matrix(child_id, V, E)
        part_padded = part_padded + jnp.einsum(
            "bcv,vo->bco", families[:, child_id], matrix, precision=lax.Precision.HIGHEST
        )
    padded = jnp.zeros((CB_DEV, channels, V + 6 * FACE), jnp.float32)
    padded = lax.dynamic_update_slice_in_dim(padded, part_padded, first_fine // 8, 0)
    face_skins = padded[:, :, V:]
    extended = extended_2(face_skins, (("brick", 0),), CB_DEV // 2)
    coarse_total = CB_DEV * owners
    offset = (neighbour - (brick_id * CB_DEV - CB_DEV // 2)) % coarse_total
    opposite = np.array([1, 0, 3, 2, 5, 4], dtype=np.int32)
    facing = extended.reshape(2 * CB_DEV, channels, 6, FACE)[:, :, opposite, :]
    selector = (
        offset[:, :, None] == jnp.arange(2 * CB_DEV, dtype=jnp.int32)[None, None, :]
    ).astype(jnp.float32)
    incoming = jnp.einsum("bke,eckf->bckf", selector, facing, precision=lax.Precision.HIGHEST)
    layer_table = jnp.asarray(layer_matrix(E))
    spread = jnp.einsum(
        "bcf,fv->bcv",
        incoming.reshape(CB_DEV, channels, 6 * FACE),
        layer_table,
        precision=lax.Precision.HIGHEST,
    )
    own_part = padded[:, :, :V] + spread
    coarse_grad = lax.psum_scatter(own_part, "tile", scatter_dimension=2, tiled=True)
    return (fine_grad, coarse_grad)


def solution(mesh):
    in_specs = (
        P(None, ("brick", "tile")),
        P(("brick", "tile")),
        P(("brick", "tile")),
        P("brick", None),
    )
    out_specs = (P(("brick", "tile"), None, None), P("brick", None, "tile"))
    return jax.shard_map(body, mesh=mesh, in_specs=in_specs, out_specs=out_specs, check_vma=False)
```

profile of v0, /device:TPU:0, one launch (start us, length us, event | category | flops | bytes accessed | tf_op | source)
XLA Modules:
  0.0 104.6 jit_solution(7585700315256930521)
XLA Ops:
  7.2 0.7 fusion.345
  7.9 0.5 convert_reduce_fusion
  8.5 1.4 %fusion.1 = pred[2048]{0:T(1024)(128)(4,1)S(1)} fusion(s32[1024]{0:T(1024)S(1)} %get-tuple-element.160), kind=kLoop, calls=%fused_computation.16 | loop fusion | flops 4192256 | bytes 6144 | tf_op jit(solution)/shard_map/reduce_or | solution.py:131
  9.9 2.6 %fusion.2 = bf16[30,2048]{1,0:T(8,128)(2,1)S(1)} fusion(s32[1024]{0:T(1024)S(1)} %get-tuple-element.160, bf16[1,1024]{1,0:T(2,128)(2,1)S(1)} %broadcast_in_dim.1181, bf16[1,1024]{1,0:T(2,128)(2,1)S(1)} %broadcast_in_dim.1180, bf16[28,1024]{1,0:T(8,128)(2,1)} %param.9), kind=kOutput, calls=%fused_computation.17 | convolution fusion | flops 128110592 | bytes 188416 | tf_op jit(solution)/shard_map/dot_general | solution.py:130
  13.1 0.8 reshape.1709
  13.9 5.2 %all-to-all-start = ((bf16[8,2,3840]{2,1,0:T(2,128)(2,1)}), bf16[8,2,3840]{2,1,0:T(2,128)(2,1)S(1)}, u32[]{:S(2)}, u32[]{:S(2)}) async-start(bf16[8,2,3840]{2,1,0:T(2,128)(2,1)} %reshape.1709), calls=%async_computation | async-start | bytes 245760 | tf_op jit(solution)/shard_map/all_to_all | solution.py:189
  20.6 3.9 %all-to-all-done = bf16[8,2,3840]{2,1,0:T(2,128)(2,1)S(1)} async-done(((bf16[8,2,3840]{2,1,0:T(2,128)(2,1)}), bf16[8,2,3840]{2,1,0:T(2,128)(2,1)S(1)}, u32[]{:S(2)}, u32[]{:S(2)}) %all-to-all-start) | async-done | bytes 122912 | tf_op jit(solution)/shard_map/all_to_all | solution.py:189
  24.8 0.8 reshape.1711
  25.6 4.9 %all-to-all-start.1 = ((bf16[4,2,7680]{2,1,0:T(2,128)(2,1)}), bf16[4,2,7680]{2,1,0:T(2,128)(2,1)S(1)}, u32[]{:S(2)}, u32[]{:S(2)}) async-start(bf16[4,2,7680]{2,1,0:T(2,128)(2,1)} %reshape.1711), calls=%async_computation.1 | async-start | bytes 245760 | tf_op jit(solution)/shard_map/all_to_all | solution.py:188
  30.6 5.8 %all-to-all-done.1 = bf16[4,2,7680]{2,1,0:T(2,128)(2,1)S(1)} async-done(((bf16[4,2,7680]{2,1,0:T(2,128)(2,1)}), bf16[4,2,7680]{2,1,0:T(2,128)(2,1)S(1)}, u32[]{:S(2)}, u32[]{:S(2)}) %all-to-all-start.1) | async-done | bytes 122912 | tf_op jit(solution)/shard_map/all_to_all | solution.py:188
  37.1 5.0 %while.16 = (s32[]{:T(128)}, f32[224,512]{1,0:T(8,128)S(1)}, s32[2048]{0:T(1024)S(1)}, bf16[28,2048]{1,0:T(8,128)(2,1)S(1)}, s32[]{:T(128)}, /*index=5*/s32[]{:T(128)}, s32[]{:T(128)}, s32[]{:T(128)}) while((s32[]{:T(128)}, f32[224,512]{1,0:T(8,128)S(1)}, s32[2048]{0:T(1024)S(1)}, bf16[28,2048]{1,0:T(8,128)(2,1)S(1)}, s32[]{:T(128)}, ...), condition=%wide.region_3.4_spmd.clone, body=%wide.region_2.3_spmd.clone.sunk | while | flops 59145480 | bytes 1428629 | solution.py:165
  38.5 0.4 convolution_add_fusion.3
  39.1 0.4 convolution_add_fusion.3
  41.5 0.4 convolution_add_fusion.3
  42.1 3.1 %fusion.101 = f32[28,896]{1,0:T(8,128)S(1)} fusion(f32[512]{0:T(512)S(1)} %get-tuple-element.245, s32[512]{0:T(512)S(1)} %get-tuple-element.249, f32[512]{0:T(512)S(1)} %get-tuple-element.241, s32[512]{0:T(512)S(1)} %get-tuple-element.250, f32[512]{0:T(512)S(1)} %get-tuple-element.246, s32[512]{0:T(512)S(1)} %get-tuple-element.251, ...), kind=kOutput, calls=%fused_computation.182 | convolution fusion | flops 164691968 | bytes 198656 | tf_op jit(solution)/shard_map/bcv,vo->bco/dot_general | solution.py:213
  45.3 3.1 %fusion.53 = f32[28,896]{1,0:T(8,128)S(1)} fusion(f32[512]{0:T(512)S(1)} %get-tuple-element.197, s32[512]{0:T(512)S(1)} %get-tuple-element.201, f32[512]{0:T(512)S(1)} %get-tuple-element.193, s32[512]{0:T(512)S(1)} %get-tuple-element.202, f32[512]{0:T(512)S(1)} %get-tuple-element.198, s32[512]{0:T(512)S(1)} %get-tuple-element.203, ...), kind=kOutput, calls=%fused_computation.134 | convolution fusion | flops 164691968 | bytes 198656 | tf_op jit(solution)/shard_map/bcv,vo->bco/dot_general | solution.py:213
  48.4 3.1 %fusion.69 = f32[28,896]{1,0:T(8,128)S(1)} fusion(f32[512]{0:T(512)S(1)} %get-tuple-element.213, s32[512]{0:T(512)S(1)} %get-tuple-element.217, f32[512]{0:T(512)S(1)} %get-tuple-element.209, s32[512]{0:T(512)S(1)} %get-tuple-element.218, f32[512]{0:T(512)S(1)} %get-tuple-element.214, s32[512]{0:T(512)S(1)} %get-tuple-element.219, ...), kind=kOutput, calls=%fused_computation.150 | convolution fusion | flops 164691968 | bytes 198656 | tf_op jit(solution)/shard_map/bcv,vo->bco/dot_general | solution.py:213
  51.5 3.3 %fusion.85 = f32[28,896]{1,0:T(8,128)S(1)} fusion(f32[512]{0:T(512)S(1)} %get-tuple-element.229, s32[512]{0:T(512)S(1)} %get-tuple-element.233, f32[512]{0:T(512)S(1)} %get-tuple-element.225, s32[512]{0:T(512)S(1)} %get-tuple-element.234, f32[512]{0:T(512)S(1)} %get-tuple-element.230, s32[512]{0:T(512)S(1)} %get-tuple-element.235, ...), kind=kOutput, calls=%fused_computation.166 | convolution fusion | flops 164691968 | bytes 198656 | tf_op jit(solution)/shard_map/bcv,vo->bco/dot_general | solution.py:213
  54.9 3.1 %fusion.21 = f32[28,896]{1,0:T(8,128)S(1)} fusion(f32[512]{0:T(512)S(1)} %get-tuple-element.181, s32[512]{0:T(512)S(1)} %get-tuple-element.185, f32[512]{0:T(512)S(1)} %get-tuple-element.177, s32[512]{0:T(512)S(1)} %get-tuple-element.186, f32[512]{0:T(512)S(1)} %get-tuple-element.182, s32[512]{0:T(512)S(1)} %get-tuple-element.187, ...), kind=kOutput, calls=%fused_computation.102 | convolution fusion | flops 164691968 | bytes 198656 | tf_op jit(solution)/shard_map/bcv,vo->bco/dot_general | solution.py:213
  58.0 3.1 %fusion.5 = f32[28,896]{1,0:T(8,128)S(1)} fusion(f32[512]{0:T(512)S(1)} %get-tuple-element.165, s32[512]{0:T(512)S(1)} %get-tuple-element.169, f32[512]{0:T(512)S(1)} %get-tuple-element.161, s32[512]{0:T(512)S(1)} %get-tuple-element.170, f32[512]{0:T(512)S(1)} %get-tuple-element.166, s32[512]{0:T(512)S(1)} %get-tuple-element.171, ...), kind=kOutput, calls=%fused_computation.86 | convolution fusion | flops 164691968 | bytes 198656 | tf_op jit(solution)/shard_map/bcv,vo->bco/dot_general | solution.py:213
  61.1 3.1 %fusion.142 = f32[28,896]{1,0:T(8,128)S(1)} fusion(f32[28,896]{1,0:T(8,128)S(1)} %fusion.53, f32[28,896]{1,0:T(8,128)S(1)} %fusion.69, f32[28,896]{1,0:T(8,128)S(1)} %fusion.85, f32[28,896]{1,0:T(8,128)S(1)} %fusion.101, f32[512]{0:T(512)S(1)} %get-tuple-element.261, s32[512]{0:T(512)S(1)} %get-tuple-element.265, f32[512]{0:T(512)S(1)} %get-tuple-element.257, ...), kind=kOutput, calls=%fused_computation.219 | convolution fusion | flops 164792320 | bytes 657408 | tf_op jit(solution)/shard_map/bcv,vo->bco/dot_general | solution.py:213
  64.3 3.4 %fusion.157 = f32[4,28,896]{2,1,0:T(8,128)S(1)} fusion(f32[4,28,896]{2,1,0:T(8,128)S(1)} %broadcast_in_dim.1183, s32[]{:T(128)S(6)} %select_n.7917, f32[28,896]{1,0:T(8,128)S(1)} %fusion.5, f32[28,896]{1,0:T(8,128)S(1)} %fusion.21, f32[28,896]{1,0:T(8,128)S(1)} %fusion.142, f32[512]{0:T(512)S(1)} %get-tuple-element.277, s32[512]{0:T(512)S(1)} %get-tuple-element.281, ...), kind=kOutput, calls=%fused_computation.224 | convolution fusion | flops 164767232 | bytes 557060 | tf_op jit(solution)/shard_map/bcv,vo->bco/dot_general | solution.py:213
  67.8 2.6 %collective-permute-start.1 = (f32[2,28,384]{2,1,0:T(8,128)S(1)}, f32[2,28,384]{2,1,0:T(8,128)S(1)}, u32[]{:S(2)}, u32[]{:S(2)}) collective-permute-start(f32[2,28,384]{2,1,0:T(8,128)S(1)} %get-tuple-element.155), channel_id=1, source_target_pairs={{4,0},{8,4},{12,8},{16,12},{20,16},{24,20},{28,24},{0,28},{5,1},{9... | collective-permute-start | bytes 258056 | tf_op jit(solution)/shard_map/ppermute | solution.py:26
  70.4 3.3 %collective-permute-done = f32[2,28,384]{2,1,0:T(8,128)S(1)} collective-permute-done((f32[2,28,384]{2,1,0:T(8,128)S(1)}, f32[2,28,384]{2,1,0:T(8,128)S(1)}, u32[]{:S(2)}, u32[]{:S(2)}) %collective-permute-start) | collective-permute-done | bytes 86048 | tf_op jit(solution)/shard_map/ppermute | solution.py:23
  73.9 0.4 copy.49
  74.3 0.6 gather_fusion
  74.9 0.5 convolution_bitcast_fusion
  75.7 0.9 copy-done
  76.6 1.3 %convolution_add_fusion.1 = f32[4,28,512]{2,1,0:T(8,128)} fusion(f32[4,28,384]{2,1,0:T(8,128)S(1)} %reshape.1706, f32[384,512,1]{1,0,2:T(8,128)S(1)} %copy-done, f32[4,28,896]{2,1,0:T(8,128)S(1)} %fusion.157), kind=kOutput, calls=%fused_computation.215 | convolution fusion | flops 264298496 | bytes 1417216 | tf_op jit(solution)/shard_map/bcf,fv->bcv/dot_general | solution.py:229
  78.0 1.0 copy.53
  79.0 17.3 %reduce-scatter.2.cloned.1.call-done = f32[4,28,128]{2,1,0:T(8,128)} async-done(((f32[4,28,512]{2,1,0:T(8,128)}), f32[4,28,128]{2,1,0:T(8,128)}) %reduce-scatter.2.cloned.1.call-update) | async-done | bytes 57360 | tf_op jit(solution)/shard_map/reduce_scatter | solution.py:236
  96.3 1.5 %copy.54 = f32[4,28,128]{2,0,1:T(4,128)} copy(f32[4,28,128]{2,1,0:T(8,128)} %reduce-scatter.2.cloned.1.call-done) | data formatting | bytes 114688
  (148 shorter events, 6.6 us)
Async XLA Ops:
  12.5 8.0 %copy-start.1 = (s32[4,6]{1,0:T(4,128)S(1)}, s32[4,6]{1,0:T(4,128)}, u32[]{:S(2)}) copy-start(s32[4,6]{1,0:T(4,128)} %param.12) | copy-start | bytes 292
  13.9 10.6 %all-to-all-start = ((bf16[8,2,3840]{2,1,0:T(2,128)(2,1)}), bf16[8,2,3840]{2,1,0:T(2,128)(2,1)S(1)}, u32[]{:S(2)}, u32[]{:S(2)}) async-start(bf16[8,2,3840]{2,1,0:T(2,128)(2,1)} %reshape.1709), calls=%async_computation | async-start | bytes 245760 | tf_op jit(solution)/shard_map/all_to_all | solution.py:189
  25.6 10.8 %all-to-all-start.1 = ((bf16[4,2,7680]{2,1,0:T(2,128)(2,1)}), bf16[4,2,7680]{2,1,0:T(2,128)(2,1)S(1)}, u32[]{:S(2)}, u32[]{:S(2)}) async-start(bf16[4,2,7680]{2,1,0:T(2,128)(2,1)} %reshape.1711), calls=%async_computation.1 | async-start | bytes 245760 | tf_op jit(solution)/shard_map/all_to_all | solution.py:188
  30.5 65.8 %reduce-scatter.2.cloned.1.call-start = ((), (), s32[]{:S(2)}) async-start(), calls=%async_computation.3 | async-start | bytes 327680 | tf_op jit(solution)/shard_map/reduce_scatter | solution.py:236
  64.3 6.1 %copy-start.2 = (s32[6]{0:T(128)S(1)}, s32[6]{0:T(128)}, u32[]{:S(2)}) copy-start(s32[6]{0:T(128)} %constant.1329) | copy-start | bytes 76
  67.7 6.0 %collective-permute-start = (f32[2,28,384]{2,1,0:T(8,128)S(1)}, f32[2,28,384]{2,1,0:T(8,128)S(1)}, u32[]{:S(2)}, u32[]{:S(2)}) collective-permute-start(f32[2,28,384]{2,1,0:T(8,128)S(1)} %get-tuple-element.154), channel_id=1, source_target_pairs={{0,4},{4,8},{8,12},{12,16},{16,20},{20,24},{24,28},{28,0},{1,5},{5... | collective-permute-start | bytes 258056 | tf_op jit(solution)/shard_map/ppermute | solution.py:23
  67.8 5.9 %collective-permute-start.1 = (f32[2,28,384]{2,1,0:T(8,128)S(1)}, f32[2,28,384]{2,1,0:T(8,128)S(1)}, u32[]{:S(2)}, u32[]{:S(2)}) collective-permute-start(f32[2,28,384]{2,1,0:T(8,128)S(1)} %get-tuple-element.155), channel_id=1, source_target_pairs={{4,0},{8,4},{12,8},{16,12},{20,16},{24,20},{28,24},{0,28},{5,1},{9... | collective-permute-start | bytes 258056 | tf_op jit(solution)/shard_map/ppermute | solution.py:26
  75.4 1.1 %copy-start = (f32[384,512,1]{1,0,2:T(8,128)S(1)}, f32[384,512,1]{1,0,2:T(8,128)}, u32[]{:S(2)}) copy-start(f32[384,512,1]{1,0,2:T(8,128)} %constant.1330) | copy-start | bytes 2359300
Sparse Core Ops, SparseCore 0:
  78.0 18.2 reduce-scatter.1
where the time goes:
time: 105 us
  matrix products  33 us (31%)
  waiting for transfers between devices  30.3 us (29%)
  between operations  14.7 us (14%)
  starting transfers between devices  12.8 us (12%)
  local copies, waits for them, and re-layouts  8.34 us (8%)
  other arithmetic  4.94 us (5%)
    dot_general x8, matrix products, body(): jnp.einsum('bcv,vo->bco', families[:, child_id], matrix, precision=lax.Pr...  25.4 us
    reduce_scatter x1, waiting for transfers between devices, body(): lax.psum_scatter(own_part, 'tile', scatter_dimension=2, tiled=True)  17.3 us
    all_to_all x1, waiting for transfers between devices, body(): lax.all_to_all(lax.all_to_all(packed.reshape(channels + 2, owners, tile_c...  5.84 us
    unnamed x12, local copies, waits for them, and re-layouts  5.53 us
    all_to_all x1, starting transfers between devices, body(): lax.all_to_all(packed.reshape(channels + 2, owners, tile_count, group_cap...  5.2 us
    all_to_all x1, starting transfers between devices, body(): lax.all_to_all(lax.all_to_all(packed.reshape(channels + 2, owners, tile_c...  4.87 us
    all_to_all x1, waiting for transfers between devices, body(): lax.all_to_all(packed.reshape(channels + 2, owners, tile_count, group_cap...  3.89 us
    ppermute x1, waiting for transfers between devices, extended_2(): lax.ppermute(lax.slice_in_dim(block, block.shape[dim] - width, None, axis...  3.26 us
  transfers between devices with their start and end apart: 5, of which 4 were waited for; matrix products, arithmetic and copies ran while one was open for 2% of the time, Pallas kernels for 0%

commit v1 on v0

--- a/solution.py
+++ b/solution.py
@@ -1,7 +1,11 @@
+import functools
+
 import jax
 import jax.numpy as jnp
 import numpy as np
 from jax import lax
+from jax.experimental import pallas as pl
+from jax.experimental.pallas import tpu as pltpu
 from jax.sharding import PartitionSpec as P
 
 E = 8
@@ -237,6 +241,334 @@
     return (fine_grad, coarse_grad)
 
 
+LANES = 128
+
+
+def tri_table():
+    below = np.arange(LANES)[:, None] < np.arange(LANES)[None, :]
+    return np.concatenate([below, np.ones((LANES, LANES), bool)], axis=1).astype(np.float32)
+
+
+def plane_weights(brick_edge):
+    table = np.zeros((2, brick_edge, brick_edge + 2), np.float32)
+    for half in range(2):
+        for cell in range(brick_edge):
+            at = half * brick_edge + cell
+            table[half, cell, at // 2 + 1] += 0.75
+            table[half, cell, at // 2 - 1 + 2 * (at % 2) + 1] += 0.25
+    return table
+
+
+def plane_matrices(brick_edge):
+    weight = plane_weights(brick_edge)
+    square = brick_edge * brick_edge
+    full = np.einsum("aym,bzn->abyzmn", weight, weight).reshape(4 * square, brick_edge + 2, brick_edge + 2)
+    out = np.zeros((4, 4 * square, 2 * LANES), np.float32)
+    last = brick_edge - 1
+    for m2 in range(-1, brick_edge + 1):
+        for m3 in range(-1, brick_edge + 1):
+            column = full[:, m2 + 1, m3 + 1]
+            out_y = m2 < 0 or m2 > last
+            out_z = m3 < 0 or m3 > last
+            cell = min(max(m2, 0), last) * brick_edge + min(max(m3, 0), last)
+            for odd in range(2):
+                if out_y == out_z:
+                    out[odd, :, odd * square + cell] += column
+                elif out_y:
+                    face = 0 if m2 < 0 else 1
+                    out[odd, :, LANES + (odd * 4 + face) * brick_edge + m3] += column
+                else:
+                    face = 2 if m3 < 0 else 3
+                    out[odd, :, LANES + (odd * 4 + face) * brick_edge + m2] += column
+            for side in range(2):
+                if out_y or out_z:
+                    out[2 + side, :, side * square + cell] += column
+                else:
+                    out[2 + side, :, LANES + square + cell] += column
+    return out
+
+
+def expand_tables(brick_edge):
+    square = brick_edge * brick_edge
+    last = brick_edge - 1
+    out = np.zeros((2, LANES, LANES), np.float32)
+    for side in range(2):
+        for odd in range(2):
+            for at in range(brick_edge):
+                base = odd * 4 * brick_edge + at
+                out[side, base, odd * square + last * brick_edge + at] = 1
+                out[side, base + brick_edge, odd * square + at] = 1
+                out[side, base + 2 * brick_edge, odd * square + at * brick_edge + last] = 1
+                out[side, base + 3 * brick_edge, odd * square + at * brick_edge] = 1
+        for cell in range(square):
+            out[side, square + cell, side * square + cell] = 1
+    return out
+
+
+def split_two(value):
+    high = value.astype(jnp.bfloat16)
+    low = (value - high.astype(jnp.float32)).astype(jnp.bfloat16)
+    return high, low
+
+
+def contract_last(left, right):
+    return lax.dot_general(left, right, (((1,), (1,)), ((), ())), preferred_element_type=jnp.float32)
+
+
+def pack_kernel(group_len, dests, brick_ref, slot_ref, grad_ref, tri_ref, out_ref, full_ref):
+    channels = grad_ref.shape[0]
+    blocks = brick_ref.shape[0]
+    square = E * E
+    brick = brick_ref[...]
+    slot = slot_ref[...]
+    bucket = brick // group_len
+    local = brick - bucket * group_len
+    plane = slot // square
+    cell = slot - plane * square
+    bucket_f = bucket.astype(jnp.float32)
+    dest_ids = lax.broadcasted_iota(jnp.int32, (dests, LANES), 0).astype(jnp.float32)
+    hots = [
+        jnp.where(jnp.broadcast_to(bucket_f[i : i + 1], (dests, LANES)) == dest_ids, 1.0, 0.0)
+        for i in range(blocks)
+    ]
+    counts = jnp.dot(
+        jnp.concatenate(hots, axis=0).astype(jnp.bfloat16), tri_ref[...], preferred_element_type=jnp.float32
+    )
+    before = jnp.zeros((dests, LANES), jnp.float32)
+    ranks = []
+    for i in range(blocks):
+        part = counts[i * dests : (i + 1) * dests]
+        ranks.append(jnp.sum(hots[i] * (part[:, :LANES] + before), axis=0, keepdims=True))
+        before = before + part[:, LANES:]
+    rank = jnp.concatenate(ranks, axis=1)
+
+    rows = lax.broadcasted_iota(jnp.int32, (4, LANES), 0)
+    local_f = (local + 1).astype(jnp.float32)
+    plane_f = plane.astype(jnp.float32)
+    cell_f = cell.astype(jnp.float32)
+    full_ref[:channels, :] = grad_ref[...]
+    for i in range(blocks):
+        code = jnp.where(
+            rows == 0,
+            local_f[i : i + 1],
+            jnp.where(rows == 1, plane_f[i : i + 1], jnp.where(rows == 2, cell_f[i : i + 1], 0.0)),
+        )
+        full_ref[channels : channels + 4, i * LANES : (i + 1) * LANES] = code.astype(jnp.bfloat16)
+    low = full_ref[:16, :]
+    high = full_ref[16:32, :]
+    bucket16 = jnp.concatenate(
+        [jnp.broadcast_to(bucket_f[i : i + 1], (16, LANES)) for i in range(blocks)], axis=1
+    ).astype(jnp.bfloat16)
+    zero = jnp.zeros_like(low)
+    low_rows = []
+    high_rows = []
+    for dest in range(dests):
+        mask = bucket16 == jnp.bfloat16(dest)
+        low_rows.append(jnp.where(mask, low, zero))
+        high_rows.append(jnp.where(mask, high, zero))
+    rank_ids = lax.broadcasted_iota(jnp.int32, (LANES, rank.shape[1]), 0).astype(jnp.float32)
+    half = LANES // 2
+    hot_low = jnp.where(rank_ids == rank, 1.0, 0.0).astype(jnp.bfloat16)
+    hot_high = jnp.where(rank_ids == rank + half, 1.0, 0.0).astype(jnp.bfloat16)
+    placed = contract_last(jnp.concatenate(low_rows, axis=0), hot_low)
+    placed = placed + contract_last(jnp.concatenate(high_rows, axis=0), hot_high)
+    out_ref[...] = placed.astype(jnp.bfloat16).reshape(dests, 16, LANES)
+
+
+def grid_kernel(channels, arrived_ref, plane_ref, fine_ref, own_ref, skin_ref, quarter_ref, turn_ref):
+    tile_id = lax.axis_index("tile")
+    sources = arrived_ref.shape[0]
+    half = LANES // 2
+    lows = []
+    highs = []
+    for p in range(sources // 2):
+        first = arrived_ref[p]
+        second = arrived_ref[p + sources // 2]
+        lows.append(jnp.concatenate([first[:, :half], second[:, :half]], axis=1))
+        highs.append(jnp.concatenate([first[:, half:], second[:, half:]], axis=1))
+    low = jnp.concatenate(lows, axis=1)
+    high = jnp.concatenate(highs, axis=1)
+    total = low.shape[1]
+    codes = high.astype(jnp.float32)
+    at = channels - 16
+    brick16 = jnp.broadcast_to(codes[at : at + 1], (16, total)).astype(jnp.bfloat16)
+    plane16 = jnp.broadcast_to(codes[at + 1 : at + 2], (16, total)).astype(jnp.bfloat16)
+    cell16 = jnp.broadcast_to(codes[at + 2 : at + 3], (16, total)).astype(jnp.bfloat16)
+    zero = jnp.zeros_like(low)
+    one = jnp.ones_like(low)
+    left = []
+    for child in range(8):
+        mask = brick16 == jnp.bfloat16(child + 1)
+        left.append(jnp.where(mask, low, zero))
+        left.append(jnp.where(mask, high, zero))
+    row_ids = lax.broadcasted_iota(jnp.int32, (16, total), 0).astype(jnp.float32)
+    cells = [
+        jnp.where(cell16 == (row_ids + 16.0 * g).astype(jnp.bfloat16), one, zero) for g in range(E * E // 16)
+    ]
+    right = []
+    for plane in range(E):
+        mask = plane16 == jnp.bfloat16(plane)
+        for g in range(E * E // 16):
+            right.append(jnp.where(mask, cells[g], zero))
+    fine = contract_last(jnp.concatenate(left, axis=0), jnp.concatenate(right, axis=0))
+    parts = [fine[32 * child : 32 * child + 32] for child in range(8)]
+    for i in range(V // LANES):
+        for child in range(8):
+            turn_ref[i, pl.ds(child, channels, stride=8), :] = parts[child][:channels, i * LANES : (i + 1) * LANES]
+        fine_ref[:, i * LANES : (i + 1) * LANES] = turn_ref[i]
+
+    lane = lax.broadcasted_iota(jnp.int32, (32, LANES), 1)
+    first_half = lane < half
+    blank = jnp.zeros((32, LANES), jnp.float32)
+
+    def slab(child, m):
+        return parts[child][:, m * LANES : (m + 1) * LANES] if 0 <= m < E // 2 else blank
+
+    def along_x(child, m):
+        value = 0.25 * jnp.where(first_half, slab(child, m + 1), slab(child, m - 1))
+        return value + 0.75 * slab(child, m) if 0 <= m < E // 2 else value
+
+    def layer(m):
+        columns = []
+        for kyz in range(4):
+            if m <= E // 2 and m >= E // 2 - 1:
+                columns.append(along_x(kyz, m) + along_x(4 + kyz, m - E // 2))
+            elif m < E // 2:
+                columns.append(along_x(kyz, m))
+            else:
+                columns.append(along_x(4 + kyz, m - E // 2))
+        return jnp.concatenate(columns, axis=1)
+
+    def matrix(which):
+        pieces = []
+        for kyz in range(4):
+            piece = plane_ref[which, kyz * half : (kyz + 1) * half, :]
+            pieces += [piece, piece]
+        return jnp.concatenate(pieces, axis=0)
+
+    def apply(stack, table):
+        high_part, low_part = split_two(stack)
+        return jnp.dot(high_part, table, preferred_element_type=jnp.float32) + jnp.dot(
+            low_part, table, preferred_element_type=jnp.float32
+        )
+
+    even = jnp.concatenate([layer(2 * q) for q in range(4)], axis=0)
+    odd = jnp.concatenate([layer(2 * q + 1) for q in range(4)], axis=0)
+    inner = apply(even, matrix(0)) + apply(odd, matrix(1))
+    below = apply(layer(-1), matrix(2))
+    above = apply(layer(E), matrix(3))
+    for q in range(4):
+        own = inner[32 * q : 32 * q + 32, :LANES]
+        skin = inner[32 * q : 32 * q + 32, LANES:]
+        if q == 0:
+            own = own + below[:, :LANES]
+            skin = skin + above[:, LANES:]
+        if q == 3:
+            own = own + above[:, :LANES]
+            skin = skin + below[:, LANES:]
+        quarter_ref[q, 0] = own
+        quarter_ref[q, 1] = skin
+    for delta in range(4):
+        own_ref[delta] = quarter_ref[tile_id ^ delta, 0][:channels]
+        skin_ref[delta] = quarter_ref[tile_id ^ delta, 1][:channels]
+
+
+def combine_kernel(channels, coarse_total, near_ref, own_ref, skin_ref, far_ref, one_ref, two_ref, three_ref,
+                   table_ref, out_ref, hold_ref):
+    tile_id = lax.axis_index("tile")
+    brick_id = lax.axis_index("brick")
+    hold_ref[tile_id, 0] = own_ref[0]
+    hold_ref[tile_id, 1] = skin_ref[0]
+    hold_ref[tile_id, 2] = far_ref[0]
+    for delta, ref in ((1, one_ref), (2, two_ref), (3, three_ref)):
+        hold_ref[tile_id ^ delta] = ref[...]
+    lane = lax.broadcasted_iota(jnp.int32, (channels, LANES), 1)
+    group = jnp.where(lane < LANES // 2, (lane // E) % 4, 4)
+    skins = [hold_ref[2, 2], hold_ref[3, 2]]
+    skins += [hold_ref[j, 1] for j in range(4)]
+    skins += [hold_ref[0, 2], hold_ref[1, 2]]
+    x_face = jnp.where(tile_id < 2, 0, 1)
+    gathered = []
+    for i in range(4):
+        near = [
+            (near_ref[i, face] - (brick_id * 4 - 2) + coarse_total) % coarse_total for face in (3, 2, 5, 4)
+        ]
+        near.append((near_ref[i, x_face] - (brick_id * 4 - 2) + coarse_total) % coarse_total)
+        source = jnp.where(
+            group == 0,
+            near[0],
+            jnp.where(group == 1, near[1], jnp.where(group == 2, near[2], jnp.where(group == 3, near[3], near[4]))),
+        )
+        first = 0 if i < 2 else 4
+        value = jnp.zeros((channels, LANES), jnp.float32)
+        for e in range(first, first + 4):
+            value = jnp.where(source == e, skins[e], value)
+        gathered.append(value)
+    table = table_ref[tile_id // 2]
+    for i in range(4):
+        high_part, low_part = split_two(gathered[i])
+        moved = jnp.dot(high_part, table, preferred_element_type=jnp.float32) + jnp.dot(
+            low_part, table, preferred_element_type=jnp.float32
+        )
+        out_ref[pl.ds(i, channels, stride=4), :] = hold_ref[i, 0] + moved
+
+
+def family_body(sample_grad, sample_brick, sample_slot, neighbour):
+    tile_count = lax.axis_size("tile")
+    owners = lax.axis_size("brick")
+    channels, samples = sample_grad.shape
+    dests = owners * tile_count
+    group_len = FB_DEV // tile_count
+    vmem = pl.BlockSpec(memory_space=pltpu.VMEM)
+    packed = pl.pallas_call(
+        functools.partial(pack_kernel, group_len, dests),
+        out_shape=jax.ShapeDtypeStruct((dests, 16, LANES), jnp.bfloat16),
+        in_specs=[vmem] * 4,
+        out_specs=vmem,
+        scratch_shapes=[pltpu.VMEM((32, samples), jnp.bfloat16)],
+        name="pack",
+    )(
+        sample_brick.reshape(samples // LANES, LANES),
+        sample_slot.reshape(samples // LANES, LANES),
+        sample_grad,
+        jnp.asarray(tri_table(), jnp.bfloat16),
+    )
+    arrived = lax.all_to_all(packed, ("brick", "tile"), 0, 0, tiled=True)
+    quarter = jax.ShapeDtypeStruct((4, channels, LANES), jnp.float32)
+    fine, own, skin = pl.pallas_call(
+        functools.partial(grid_kernel, channels),
+        out_shape=(jax.ShapeDtypeStruct((channels * 8, V), jnp.float32), quarter, quarter),
+        in_specs=[vmem] * 2,
+        out_specs=(vmem,) * 3,
+        scratch_shapes=[
+            pltpu.VMEM((4, 2, 32, LANES), jnp.float32),
+            pltpu.VMEM((V // LANES, channels * 8, LANES), jnp.float32),
+        ],
+        name="grid",
+    )(arrived, jnp.asarray(plane_matrices(E), jnp.bfloat16))
+    pairs = []
+    for b in range(owners):
+        for t in range(tile_count):
+            step = 1 if t >= tile_count // 2 else -1
+            pairs.append((b * tile_count + t, (b + step) % owners * tile_count + t))
+    far = lax.ppermute(skin, ("brick", "tile"), pairs)
+    arrivals = []
+    for delta in (3, 2, 1):
+        message = jnp.stack([own[delta], skin[delta], far[delta]])
+        arrivals.append(lax.ppermute(message, "tile", [(t, t ^ delta) for t in range(tile_count)]))
+    coarse = pl.pallas_call(
+        functools.partial(combine_kernel, channels, CB_DEV * owners),
+        out_shape=jax.ShapeDtypeStruct((channels * CB_DEV, LANES), jnp.float32),
+        in_specs=[pl.BlockSpec(memory_space=pltpu.SMEM)] + [vmem] * 7,
+        out_specs=vmem,
+        scratch_shapes=[pltpu.VMEM((4, 3, channels, LANES), jnp.float32)],
+        name="combine",
+    )(neighbour, own, skin, far, arrivals[2], arrivals[1], arrivals[0], jnp.asarray(expand_tables(E), jnp.bfloat16))
+    fine_grad = fine.reshape(channels, 8, V).transpose(1, 0, 2)
+    coarse_grad = coarse.reshape(channels, CB_DEV, LANES).transpose(1, 0, 2)
+    return fine_grad, coarse_grad
+
+
 def solution(mesh):
     in_specs = (
         P(None, ("brick", "tile")),
@@ -245,4 +577,16 @@
         P("brick", None),
     )
     out_specs = (P(("brick", "tile"), None, None), P("brick", None, "tile"))
-    return jax.shard_map(body, mesh=mesh, in_specs=in_specs, out_specs=out_specs, check_vma=False)
+
+    def step(sample_grad, sample_brick, sample_slot, neighbour):
+        owners, tile_count = mesh.shape["brick"], mesh.shape["tile"]
+        samples = sample_grad.shape[1] // (owners * tile_count)
+        whole_family = FB_DEV == 8 * tile_count == 2 * 4 * CB_DEV and tile_count == CB_DEV
+        full_messages = 2 * samples == (LANES // 2) * owners * tile_count and samples % LANES == 0
+        fits = whole_family and full_messages and sample_grad.shape[0] == 28 and owners > 2
+        chosen = family_body if fits else body
+        return jax.shard_map(chosen, mesh=mesh, in_specs=in_specs, out_specs=out_specs, check_vma=False)(
+            sample_grad, sample_brick, sample_slot, neighbour
+        )
+
+    return step

time: 105 us -> 38 us (0.36)
  matrix products: 33 us -> 0 us
  waiting for transfers between devices: 30.3 us -> 7.15 us
  blocking collectives: 0 us -> 15.8 us
  between operations: 14.7 us -> 0.64 us
  starting transfers between devices: 12.8 us -> 4.48 us
  Pallas kernels: 0 us -> 7.49 us
  local copies, waits for them, and re-layouts: 8.34 us -> 2.05 us
  other arithmetic: 4.94 us -> 0.02 us
    dot_general x19 -> x0, matrix products: 33 us -> none  [the longest x8 25.4 us: body(): jnp.einsum('bcv,vo->bco', families[:, child_id], matrix, precision=lax.Pr...]
    reduce_scatter x1 -> x0, waiting for transfers between devices: 17.3 us -> none  [body(): lax.psum_scatter(own_part, 'tile', scatter_dimension=2, tiled=True)]
    all_to_all x0 -> x1, blocking collectives: none -> 15.8 us  [family_body(): arrived = lax.all_to_all(packed, ('brick', 'tile'), 0, 0, tiled=True)]
    all_to_all x2 -> x0, starting transfers between devices: 10.1 us -> none  [the longest x1 5.2 us: body(): lax.all_to_all(packed.reshape(channels + 2, owners, tile_count, group_cap...]
    all_to_all x2 -> x0, waiting for transfers between devices: 9.73 us -> none  [the longest x1 5.84 us: body(): lax.all_to_all(lax.all_to_all(packed.reshape(channels + 2, owners, tile_c...]
    pallas_call x0 -> x3, Pallas kernels: none -> 7.49 us  [the longest x1 3.13 us: family_body(): pl.pallas_call(functools.partial(grid_kernel, channels), out_shape=(jax.S...]
    unnamed x12 -> x8, local copies, waits for them, and re-layouts: 5.53 us -> 1.24 us
    ppermute x2 -> x4, waiting for transfers between devices: 3.26 us -> 7.15 us  [the longest x3 5.74 us: family_body(): lax.ppermute(message, 'tile', [(t, t ^ delta) for t in range(tile_count)])]
  transfers between devices with their start and end apart: 5 -> 4, of which waited for: 4 -> 4; matrix products, arithmetic and copies ran while one was open for 2% -> 2% of each run, Pallas kernels for 0% -> 0%
where the time goes in v1:
time: 38 us; the launch traced here: 37.7 us
  blocking collectives  15.8 us (42%)
  Pallas kernels  7.49 us (20%)
  waiting for transfers between devices  7.15 us (19%)
  starting transfers between devices  4.48 us (12%)
  local copies, waits for them, and re-layouts  2.05 us (5%)
  between operations  0.64 us (2%)
    all_to_all x1, blocking collectives, family_body(): arrived = lax.all_to_all(packed, ('brick', 'tile'), 0, 0, tiled=True)  15.8 us
    ppermute x3, waiting for transfers between devices, family_body(): lax.ppermute(message, 'tile', [(t, t ^ delta) for t in range(tile_count)])  5.74 us
    ppermute x3, starting transfers between devices, family_body(): lax.ppermute(message, 'tile', [(t, t ^ delta) for t in range(tile_count)])  4.48 us
    pallas_call x1, Pallas kernels, family_body(): pl.pallas_call(functools.partial(grid_kernel, channels), out_shape=(jax.S...  3.13 us
    pallas_call x1, Pallas kernels, family_body(): pl.pallas_call(functools.partial(pack_kernel, group_len, dests), out_shap...  2.49 us
    pallas_call x1, Pallas kernels, family_body(): pl.pallas_call(functools.partial(combine_kernel, channels, CB_DEV * owner...  1.87 us
    ppermute x1, waiting for transfers between devices, family_body(): far = lax.ppermute(skin, ('brick', 'tile'), pairs)  1.41 us
    unnamed x8, local copies, waits for them, and re-layouts  1.24 us
  transfers between devices with their start and end apart: 4, of which 4 were waited for; matrix products, arithmetic and copies ran while one was open for 2% of the time, Pallas kernels for 0%

profile of v1, /device:TPU:0, one launch (start us, length us, event | category | flops | bytes accessed | tf_op | source)
XLA Modules:
  0.0 37.7 jit_solution(15403831572909040023)
XLA Ops:
  0.6 2.5 %pack.1 = bf16[32,16,128]{2,1,0:T(8,128)(2,1)} custom-call(s32[8,128]{1,0:T(8,128)} %bitcast.9, s32[8,128]{1,0:T(8,128)} %bitcast.10, bf16[28,1024]{1,0:T(8,128)(2,1)} %grad_ref.1, bf16[128,256]{1,0:T(8,128)(2,1)} %constant.6.clone.tri_ref), custom_call_target="tpu_custom_call" | custom-call | tf_op jit(solution)/shard_map/pack/pallas_call | solution.py:523
  3.1 15.8 %all_to_all.5.arrived_ref = bf16[32,16,128]{2,1,0:T(8,128)(2,1)} all-to-all(bf16[32,16,128]{2,1,0:T(8,128)(2,1)} %pack.1), channel_id=1, replica_groups=mesh['brick'=8,'tile'=4] {'brick','tile'}, dimensions={0} | all-to-all | bytes 262144 | tf_op jit(solution)/shard_map/all_to_all | solution.py:536
  18.9 3.1 %grid.1 = (f32[224,512]{1,0:T(8,128)}, f32[4,28,128]{2,1,0:T(8,128)}, f32[4,28,128]{2,1,0:T(8,128)}) custom-call(bf16[32,16,128]{2,1,0:T(8,128)(2,1)} %all_to_all.5.arrived_ref, bf16[4,256,256]{2,1,0:T(8,128)(2,1)} %constant.7.clone.plane_ref), custom_call_target="tpu_custom_call" | custom-call | tf_op jit(solution)/shard_map/grid/pallas_call | solution.py:538
  22.1 0.0 collective-permute-start
  22.1 0.8 %fusion = (f32[1,28,128]{2,1,0:T(8,128)S(1)}, f32[1,28,128]{2,1,0:T(8,128)S(1)}, f32[1,28,128]{2,1,0:T(8,128)S(1)}, f32[1,28,128]{2,1,0:T(8,128)S(1)}, f32[1,28,128]{2,1,0:T(8,128)S(1)}, /*index=5*/f32[1,28,128]{2,1,0:T(8,128)S(1)}) fusion(f32[4,28,128]{2,1,0:T(8,128)} %get-tuple-element.6.own_ref, f32[4,28,128]{2,1,0:T(8,128)} %get-tuple-element.7.skin_ref), kind=kLoop, calls=%fused_computation.3 | loop fusion | bytes 172032 | tf_op jit(solution)/shard_map/slice | solution.py:557
  22.9 1.4 %collective-permute-done.far_ref = f32[4,28,128]{2,1,0:T(8,128)S(1)} collective-permute-done((f32[4,28,128]{2,1,0:T(8,128)}, f32[4,28,128]{2,1,0:T(8,128)S(1)}, u32[]{:S(2)}, u32[]{:S(2)}) %collective-permute-start) | collective-permute-done | bytes 57376 | tf_op jit(solution)/shard_map/ppermute | solution.py:554
  24.3 0.0 copy-start
  24.3 0.6 %copy-done = f32[4,28,128]{2,1,0:T(8,128)} copy-done((f32[4,28,128]{2,1,0:T(8,128)}, f32[4,28,128]{2,1,0:T(8,128)S(1)}, u32[]{:S(2)}) %copy-start) | copy-done | bytes 57368
  24.9 0.7 %collective-permute-start.1 = (f32[3,28,128]{2,1,0:T(8,128)S(1)}, f32[3,28,128]{2,1,0:T(8,128)S(1)}, u32[]{:S(2)}, u32[]{:S(2)}) collective-permute-start(f32[3,28,128]{2,1,0:T(8,128)S(1)} %pad_maximum_fusion), channel_id=1, source_target_pairs={{0,1},{1,0},{2,3},{3,2},{4,5},{5,4},{6,7},{7,6},{8,9},{9,8},{10,11... | collective-permute-start | bytes 129032 | tf_op jit(solution)/shard_map/ppermute | solution.py:558
  25.6 3.7 %collective-permute-start.2 = (f32[3,28,128]{2,1,0:T(8,128)S(1)}, f32[3,28,128]{2,1,0:T(8,128)S(1)}, u32[]{:S(2)}, u32[]{:S(2)}) collective-permute-start(f32[3,28,128]{2,1,0:T(8,128)S(1)} %pad_maximum_fusion.1), channel_id=1, source_target_pairs={{0,2},{1,3},{2,0},{3,1},{4,6},{5,7},{6,4},{7,5},{8,10},{9,11},{10,... | collective-permute-start | bytes 129032 | tf_op jit(solution)/shard_map/ppermute | solution.py:558
  29.3 0.1 collective-permute-start.3
  29.4 0.1 collective-permute-done.1.one_ref
  29.5 0.0 copy-start.1
  29.5 3.8 %collective-permute-done.2.two_ref = f32[3,28,128]{2,1,0:T(8,128)S(1)} collective-permute-done((f32[3,28,128]{2,1,0:T(8,128)S(1)}, f32[3,28,128]{2,1,0:T(8,128)S(1)}, u32[]{:S(2)}, u32[]{:S(2)}) %collective-permute-start.2) | collective-permute-done | bytes 43040 | tf_op jit(solution)/shard_map/ppermute | solution.py:558
  33.3 0.0 copy-start.2
  33.3 1.9 %collective-permute-done.3.three_ref = f32[3,28,128]{2,1,0:T(8,128)S(1)} collective-permute-done((f32[3,28,128]{2,1,0:T(8,128)S(1)}, f32[3,28,128]{2,1,0:T(8,128)S(1)}, u32[]{:S(2)}, u32[]{:S(2)}) %collective-permute-start.3) | collective-permute-done | bytes 43040 | tf_op jit(solution)/shard_map/ppermute | solution.py:558
  35.2 0.0 copy-done.1
  35.2 0.0 copy-done.2
  35.2 0.0 copy-start.3
  35.2 0.6 %copy-done.3 = f32[3,28,128]{2,1,0:T(8,128)} copy-done((f32[3,28,128]{2,1,0:T(8,128)}, f32[3,28,128]{2,1,0:T(8,128)S(1)}, u32[]{:S(2)}) %copy-start.3) | copy-done | bytes 43032
  35.8 1.9 %combine.1 = f32[112,128]{1,0:T(8,128)} custom-call(s32[4,6]{1,0:T(4,128)} %near_ref.1, f32[4,28,128]{2,1,0:T(8,128)} %get-tuple-element.6.own_ref, f32[4,28,128]{2,1,0:T(8,128)} %get-tuple-element.7.skin_ref, f32[4,28,128]{2,1,0:T(8,128)} %copy-done, f32[3,28,128]{2,1,0:T(8,128)} %copy-done.1, f32[3,28,128]{2,1,0:T(8,128)} %copy-done.2, ...), custom_call_target="tpu_custom_call" | custom-call | tf_op jit(solution)/shard_map/combine/pallas_call | solution.py:559
  (4 shorter events, 0.0 us)
Async XLA Ops:
  22.1 2.2 %collective-permute-start = (f32[4,28,128]{2,1,0:T(8,128)}, f32[4,28,128]{2,1,0:T(8,128)S(1)}, u32[]{:S(2)}, u32[]{:S(2)}) collective-permute-start(f32[4,28,128]{2,1,0:T(8,128)} %get-tuple-element.7.skin_ref), channel_id=1, source_target_pairs={{0,28},{1,29},{2,6},{3,7},{4,0},{5,1},{6,10},{7,11},{8,4},{9,5},{1... | collective-permute-start | bytes 172040 | tf_op jit(solution)/shard_map/ppermute | solution.py:554
  24.3 0.6 %copy-start = (f32[4,28,128]{2,1,0:T(8,128)}, f32[4,28,128]{2,1,0:T(8,128)S(1)}, u32[]{:S(2)}) copy-start(f32[4,28,128]{2,1,0:T(8,128)S(1)} %collective-permute-done.far_ref) | copy-start | bytes 172036
  24.9 4.6 %collective-permute-start.1 = (f32[3,28,128]{2,1,0:T(8,128)S(1)}, f32[3,28,128]{2,1,0:T(8,128)S(1)}, u32[]{:S(2)}, u32[]{:S(2)}) collective-permute-start(f32[3,28,128]{2,1,0:T(8,128)S(1)} %pad_maximum_fusion), channel_id=1, source_target_pairs={{0,1},{1,0},{2,3},{3,2},{4,5},{5,4},{6,7},{7,6},{8,9},{9,8},{10,11... | collective-permute-start | bytes 129032 | tf_op jit(solution)/shard_map/ppermute | solution.py:558
  25.6 7.7 %collective-permute-start.2 = (f32[3,28,128]{2,1,0:T(8,128)S(1)}, f32[3,28,128]{2,1,0:T(8,128)S(1)}, u32[]{:S(2)}, u32[]{:S(2)}) collective-permute-start(f32[3,28,128]{2,1,0:T(8,128)S(1)} %pad_maximum_fusion.1), channel_id=1, source_target_pairs={{0,2},{1,3},{2,0},{3,1},{4,6},{5,7},{6,4},{7,5},{8,10},{9,11},{10,... | collective-permute-start | bytes 129032 | tf_op jit(solution)/shard_map/ppermute | solution.py:558
  29.3 5.9 %collective-permute-start.3 = (f32[3,28,128]{2,1,0:T(8,128)S(1)}, f32[3,28,128]{2,1,0:T(8,128)S(1)}, u32[]{:S(2)}, u32[]{:S(2)}) collective-permute-start(f32[3,28,128]{2,1,0:T(8,128)S(1)} %pad_maximum_fusion.2), channel_id=1, source_target_pairs={{0,3},{1,2},{2,1},{3,0},{4,7},{5,6},{6,5},{7,4},{8,11},{9,10},{10,... | collective-permute-start | bytes 129032 | tf_op jit(solution)/shard_map/ppermute | solution.py:558
  29.5 5.7 %copy-start.1 = (f32[3,28,128]{2,1,0:T(8,128)}, f32[3,28,128]{2,1,0:T(8,128)S(1)}, u32[]{:S(2)}) copy-start(f32[3,28,128]{2,1,0:T(8,128)S(1)} %collective-permute-done.1.one_ref) | copy-start | bytes 129028
  33.3 1.9 %copy-start.2 = (f32[3,28,128]{2,1,0:T(8,128)}, f32[3,28,128]{2,1,0:T(8,128)S(1)}, u32[]{:S(2)}) copy-start(f32[3,28,128]{2,1,0:T(8,128)S(1)} %collective-permute-done.2.two_ref) | copy-start | bytes 129028
  35.2 0.6 %copy-start.3 = (f32[3,28,128]{2,1,0:T(8,128)}, f32[3,28,128]{2,1,0:T(8,128)S(1)}, u32[]{:S(2)}) copy-start(f32[3,28,128]{2,1,0:T(8,128)S(1)} %collective-permute-done.3.three_ref) | copy-start | bytes 129028

commit v2 on v1

--- a/solution.py
+++ b/solution.py
@@ -7,6 +7,7 @@
 from jax.experimental import pallas as pl
 from jax.experimental.pallas import tpu as pltpu
 from jax.sharding import PartitionSpec as P
+
 
 E = 8
 V = 512
@@ -242,11 +243,7 @@
 
 
 LANES = 128
-
-
-def tri_table():
-    below = np.arange(LANES)[:, None] < np.arange(LANES)[None, :]
-    return np.concatenate([below, np.ones((LANES, LANES), bool)], axis=1).astype(np.float32)
+KERNEL_VMEM = 16 * 1024 * 1024
 
 
 def plane_weights(brick_edge):
@@ -315,10 +312,23 @@
     return lax.dot_general(left, right, (((1,), (1,)), ((), ())), preferred_element_type=jnp.float32)
 
 
-def pack_kernel(group_len, dests, brick_ref, slot_ref, grad_ref, tri_ref, out_ref, full_ref):
-    channels = grad_ref.shape[0]
+def pack_kernel(group_len, dests, brick_hbm, slot_hbm, grad_hbm, plane_hbm, out_ref, plane_ref, brick_ref, slot_ref, grad_ref, high_ref, sems):
+    channels = grad_hbm.shape[0]
     blocks = brick_ref.shape[0]
     square = E * E
+    copies = [
+        pltpu.make_async_copy(brick_hbm, brick_ref, sems.at[0]),
+        pltpu.make_async_copy(slot_hbm, slot_ref, sems.at[1]),
+        pltpu.make_async_copy(grad_hbm, grad_ref, sems.at[2]),
+        pltpu.make_async_copy(plane_hbm, plane_ref, sems.at[3]),
+    ]
+    for copy in copies:
+        copy.start()
+    at_row = lax.broadcasted_iota(jnp.int32, (LANES, 2 * LANES), 0)
+    at_lane = lax.broadcasted_iota(jnp.int32, (LANES, 2 * LANES), 1)
+    tri = jnp.where((at_row < at_lane) | (at_lane >= LANES), 1.0, 0.0).astype(jnp.bfloat16)
+    copies[0].wait()
+    copies[1].wait()
     brick = brick_ref[...]
     slot = slot_ref[...]
     bucket = brick // group_len
@@ -332,7 +342,7 @@
         for i in range(blocks)
     ]
     counts = jnp.dot(
-        jnp.concatenate(hots, axis=0).astype(jnp.bfloat16), tri_ref[...], preferred_element_type=jnp.float32
+        jnp.concatenate(hots, axis=0).astype(jnp.bfloat16), tri, preferred_element_type=jnp.float32
     )
     before = jnp.zeros((dests, LANES), jnp.float32)
     ranks = []
@@ -346,16 +356,17 @@
     local_f = (local + 1).astype(jnp.float32)
     plane_f = plane.astype(jnp.float32)
     cell_f = cell.astype(jnp.float32)
-    full_ref[:channels, :] = grad_ref[...]
     for i in range(blocks):
         code = jnp.where(
             rows == 0,
             local_f[i : i + 1],
             jnp.where(rows == 1, plane_f[i : i + 1], jnp.where(rows == 2, cell_f[i : i + 1], 0.0)),
         )
-        full_ref[channels : channels + 4, i * LANES : (i + 1) * LANES] = code.astype(jnp.bfloat16)
-    low = full_ref[:16, :]
-    high = full_ref[16:32, :]
+        high_ref[channels - 16 : channels - 12, i * LANES : (i + 1) * LANES] = code.astype(jnp.bfloat16)
+    copies[2].wait()
+    high_ref[: channels - 16, :] = grad_ref[16:channels, :]
+    low = grad_ref[:16, :]
+    high = high_ref[...]
     bucket16 = jnp.concatenate(
         [jnp.broadcast_to(bucket_f[i : i + 1], (16, LANES)) for i in range(blocks)], axis=1
     ).astype(jnp.bfloat16)
@@ -373,9 +384,10 @@
     placed = contract_last(jnp.concatenate(low_rows, axis=0), hot_low)
     placed = placed + contract_last(jnp.concatenate(high_rows, axis=0), hot_high)
     out_ref[...] = placed.astype(jnp.bfloat16).reshape(dests, 16, LANES)
-
-
-def grid_kernel(channels, arrived_ref, plane_ref, fine_ref, own_ref, skin_ref, quarter_ref, turn_ref):
+    copies[3].wait()
+
+
+def grid_kernel(channels, arrived_ref, plane_ref, fine_ref, own_ref, skin_ref, quarter_ref):
     tile_id = lax.axis_index("tile")
     sources = arrived_ref.shape[0]
     half = LANES // 2
@@ -412,10 +424,7 @@
             right.append(jnp.where(mask, cells[g], zero))
     fine = contract_last(jnp.concatenate(left, axis=0), jnp.concatenate(right, axis=0))
     parts = [fine[32 * child : 32 * child + 32] for child in range(8)]
-    for i in range(V // LANES):
-        for child in range(8):
-            turn_ref[i, pl.ds(child, channels, stride=8), :] = parts[child][:channels, i * LANES : (i + 1) * LANES]
-        fine_ref[:, i * LANES : (i + 1) * LANES] = turn_ref[i]
+    fine_ref[...] = fine
 
     lane = lax.broadcasted_iota(jnp.int32, (32, LANES), 1)
     first_half = lane < half
@@ -473,32 +482,39 @@
         skin_ref[delta] = quarter_ref[tile_id ^ delta, 1][:channels]
 
 
-def combine_kernel(channels, coarse_total, near_ref, own_ref, skin_ref, far_ref, one_ref, two_ref, three_ref,
+def turn_kernel(channels, coarse_total, rows_ref, near_ref, fine_ref, source_ref, turn_ref):
+    first = lax.axis_index("brick") * CB_DEV - CB_DEV // 2
+    lane = lax.broadcasted_iota(jnp.int32, (8, LANES), 1)
+    group = jnp.where(lane < LANES // 2, (lane // E) % 4, 4)
+    x_face = jnp.where(lax.axis_index("tile") < 2, 0, 1)
+    for i in range(CB_DEV):
+        near = [(near_ref[i, face] - first + coarse_total) % coarse_total for face in (3, 2, 5, 4, x_face)]
+        source = jnp.where(group == 0, near[0], near[1])
+        for k in range(2, 5):
+            source = jnp.where(group == k, near[k], source)
+        source_ref[i] = source
+    for i in range(V // LANES):
+        for child in range(8):
+            turn_ref[i, pl.ds(child, channels, stride=8), :] = rows_ref[
+                32 * child : 32 * child + channels, i * LANES : (i + 1) * LANES
+            ]
+        fine_ref[:, i * LANES : (i + 1) * LANES] = turn_ref[i]
+
+
+def combine_kernel(channels, source_ref, own_ref, skin_ref, far_ref, one_ref, two_ref, three_ref,
                    table_ref, out_ref, hold_ref):
     tile_id = lax.axis_index("tile")
-    brick_id = lax.axis_index("brick")
     hold_ref[tile_id, 0] = own_ref[0]
     hold_ref[tile_id, 1] = skin_ref[0]
     hold_ref[tile_id, 2] = far_ref[0]
     for delta, ref in ((1, one_ref), (2, two_ref), (3, three_ref)):
         hold_ref[tile_id ^ delta] = ref[...]
-    lane = lax.broadcasted_iota(jnp.int32, (channels, LANES), 1)
-    group = jnp.where(lane < LANES // 2, (lane // E) % 4, 4)
     skins = [hold_ref[2, 2], hold_ref[3, 2]]
     skins += [hold_ref[j, 1] for j in range(4)]
     skins += [hold_ref[0, 2], hold_ref[1, 2]]
-    x_face = jnp.where(tile_id < 2, 0, 1)
     gathered = []
     for i in range(4):
-        near = [
-            (near_ref[i, face] - (brick_id * 4 - 2) + coarse_total) % coarse_total for face in (3, 2, 5, 4)
-        ]
-        near.append((near_ref[i, x_face] - (brick_id * 4 - 2) + coarse_total) % coarse_total)
-        source = jnp.where(
-            group == 0,
-            near[0],
-            jnp.where(group == 1, near[1], jnp.where(group == 2, near[2], jnp.where(group == 3, near[3], near[4]))),
-        )
+        source = jnp.broadcast_to(source_ref[i, :1], (channels, LANES))
         first = 0 if i < 2 else 4
         value = jnp.zeros((channels, LANES), jnp.float32)
         for e in range(first, first + 4):
@@ -520,50 +536,71 @@
     dests = owners * tile_count
     group_len = FB_DEV // tile_count
     vmem = pl.BlockSpec(memory_space=pltpu.VMEM)
-    packed = pl.pallas_call(
+    packed, planes = pl.pallas_call(
         functools.partial(pack_kernel, group_len, dests),
-        out_shape=jax.ShapeDtypeStruct((dests, 16, LANES), jnp.bfloat16),
-        in_specs=[vmem] * 4,
-        out_specs=vmem,
-        scratch_shapes=[pltpu.VMEM((32, samples), jnp.bfloat16)],
+        out_shape=(
+            jax.ShapeDtypeStruct((dests, 16, LANES), jnp.bfloat16),
+            jax.ShapeDtypeStruct((4, 4 * E * E, 2 * LANES), jnp.bfloat16),
+        ),
+        in_specs=[pl.BlockSpec(memory_space=pltpu.HBM)] * 4,
+        out_specs=(vmem, vmem),
+        scratch_shapes=[
+            pltpu.VMEM((samples // LANES, LANES), jnp.int32),
+            pltpu.VMEM((samples // LANES, LANES), jnp.int32),
+            pltpu.VMEM((channels, samples), jnp.bfloat16),
+            pltpu.VMEM((16, samples), jnp.bfloat16),
+            pltpu.SemaphoreType.DMA((4,)),
+        ],
+        compiler_params=pltpu.CompilerParams(vmem_limit_bytes=KERNEL_VMEM),
         name="pack",
     )(
-        sample_brick.reshape(samples // LANES, LANES),
-        sample_slot.reshape(samples // LANES, LANES),
-        sample_grad,
-        jnp.asarray(tri_table(), jnp.bfloat16),
+        pltpu.with_memory_space_constraint(sample_brick.reshape(samples // LANES, LANES), pltpu.HBM),
+        pltpu.with_memory_space_constraint(sample_slot.reshape(samples // LANES, LANES), pltpu.HBM),
+        pltpu.with_memory_space_constraint(sample_grad, pltpu.HBM),
+        pltpu.with_memory_space_constraint(jnp.asarray(plane_matrices(E), jnp.bfloat16), pltpu.HBM),
     )
     arrived = lax.all_to_all(packed, ("brick", "tile"), 0, 0, tiled=True)
     quarter = jax.ShapeDtypeStruct((4, channels, LANES), jnp.float32)
-    fine, own, skin = pl.pallas_call(
+    rows, own, skin = pl.pallas_call(
         functools.partial(grid_kernel, channels),
-        out_shape=(jax.ShapeDtypeStruct((channels * 8, V), jnp.float32), quarter, quarter),
-        in_specs=[vmem] * 2,
+        out_shape=(jax.ShapeDtypeStruct((8 * 32, V), jnp.float32), quarter, quarter),
+        in_specs=[vmem, vmem],
         out_specs=(vmem,) * 3,
-        scratch_shapes=[
-            pltpu.VMEM((4, 2, 32, LANES), jnp.float32),
-            pltpu.VMEM((V // LANES, channels * 8, LANES), jnp.float32),
-        ],
+        scratch_shapes=[pltpu.VMEM((4, 2, 32, LANES), jnp.float32)],
+        compiler_params=pltpu.CompilerParams(vmem_limit_bytes=KERNEL_VMEM),
         name="grid",
-    )(arrived, jnp.asarray(plane_matrices(E), jnp.bfloat16))
+    )(arrived, planes)
     pairs = []
     for b in range(owners):
         for t in range(tile_count):
             step = 1 if t >= tile_count // 2 else -1
             pairs.append((b * tile_count + t, (b + step) % owners * tile_count + t))
     far = lax.ppermute(skin, ("brick", "tile"), pairs)
-    arrivals = []
+    fine, source = pl.pallas_call(
+        functools.partial(turn_kernel, channels, CB_DEV * owners),
+        out_shape=(
+            jax.ShapeDtypeStruct((channels * 8, V), jnp.float32),
+            jax.ShapeDtypeStruct((CB_DEV, 8, LANES), jnp.int32),
+        ),
+        in_specs=[vmem, pl.BlockSpec(memory_space=pltpu.SMEM)],
+        out_specs=(vmem, vmem),
+        scratch_shapes=[pltpu.VMEM((V // LANES, channels * 8, LANES), jnp.float32)],
+        compiler_params=pltpu.CompilerParams(vmem_limit_bytes=KERNEL_VMEM),
+        name="turn",
+    )(rows, neighbour)
+    arrivals = {}
     for delta in (3, 2, 1):
         message = jnp.stack([own[delta], skin[delta], far[delta]])
-        arrivals.append(lax.ppermute(message, "tile", [(t, t ^ delta) for t in range(tile_count)]))
+        arrivals[delta] = lax.ppermute(message, "tile", [(t, t ^ delta) for t in range(tile_count)])
     coarse = pl.pallas_call(
-        functools.partial(combine_kernel, channels, CB_DEV * owners),
+        functools.partial(combine_kernel, channels),
         out_shape=jax.ShapeDtypeStruct((channels * CB_DEV, LANES), jnp.float32),
-        in_specs=[pl.BlockSpec(memory_space=pltpu.SMEM)] + [vmem] * 7,
+        in_specs=[vmem] * 8,
         out_specs=vmem,
         scratch_shapes=[pltpu.VMEM((4, 3, channels, LANES), jnp.float32)],
+        compiler_params=pltpu.CompilerParams(vmem_limit_bytes=KERNEL_VMEM),
         name="combine",
-    )(neighbour, own, skin, far, arrivals[2], arrivals[1], arrivals[0], jnp.asarray(expand_tables(E), jnp.bfloat16))
+    )(source, own, skin, far, arrivals[1], arrivals[2], arrivals[3], jnp.asarray(expand_tables(E), jnp.bfloat16))
     fine_grad = fine.reshape(channels, 8, V).transpose(1, 0, 2)
     coarse_grad = coarse.reshape(channels, CB_DEV, LANES).transpose(1, 0, 2)
     return fine_grad, coarse_grad
@@ -584,9 +621,10 @@
         whole_family = FB_DEV == 8 * tile_count == 2 * 4 * CB_DEV and tile_count == CB_DEV
         full_messages = 2 * samples == (LANES // 2) * owners * tile_count and samples % LANES == 0
         fits = whole_family and full_messages and sample_grad.shape[0] == 28 and owners > 2
-        chosen = family_body if fits else body
-        return jax.shard_map(chosen, mesh=mesh, in_specs=in_specs, out_specs=out_specs, check_vma=False)(
-            sample_grad, sample_brick, sample_slot, neighbour
-        )
+        if not fits:
+            mapped = jax.shard_map(body, mesh=mesh, in_specs=in_specs, out_specs=out_specs, check_vma=False)
+        else:
+            mapped = jax.shard_map(family_body, mesh=mesh, in_specs=in_specs, out_specs=out_specs, check_vma=False)
+        return mapped(sample_grad, sample_brick, sample_slot, neighbour)
 
     return step

time: 38 us -> 32.6 us (0.86)
  Pallas kernels: 7.49 us -> 5.28 us
  local copies, waits for them, and re-layouts: 2.05 us -> 0.56 us
  waiting for transfers between devices: 7.15 us -> 5.67 us
    ppermute x3, waiting for transfers between devices: 5.74 us -> 3.79 us  [family_body(): lax.ppermute(message, 'tile', [(t, t ^ delta) for t in range(tile_count)])]
    pallas_call x1, Pallas kernels: 3.13 us -> 1.27 us  [family_body(): pl.pallas_call(functools.partial(grid_kernel, channels), out_shape=(jax.S...]
    pallas_call x1, Pallas kernels: 2.49 us -> 1.69 us  [family_body(): pl.pallas_call(functools.partial(pack_kernel, group_len, dests), out_shap...]
    slice x2, local copies, waits for them, and re-layouts: 0.82 us -> 0.01 us  [family_body(): message = jnp.stack([own[delta], skin[delta], far[delta]])]
    unnamed x8 -> x4, local copies, waits for them, and re-layouts: 1.24 us -> 0.55 us
    ppermute x1, waiting for transfers between devices: 1.41 us -> 1.88 us  [family_body(): far = lax.ppermute(skin, ('brick', 'tile'), pairs)]
    pallas_call x1 -> x2, Pallas kernels: 1.87 us -> 2.32 us  [the longest x1 1.49 us: family_body(): pl.pallas_call(functools.partial(turn_kernel, channels, CB_DEV * owners),...]
  transfers between devices with their start and end apart: 4 -> 4, of which waited for: 4 -> 3; matrix products, arithmetic and copies ran while one was open for 2% -> 0% of each run, Pallas kernels for 0% -> 5%
where the time goes in v2:
time: 32.6 us; the launch traced here: 32.4 us
  blocking collectives  15.5 us (48%)
  waiting for transfers between devices  5.67 us (17%)
  Pallas kernels  5.28 us (16%)
  starting transfers between devices  4.69 us (14%)
  between operations  0.68 us (2%)
  local copies, waits for them, and re-layouts  0.56 us (2%)
    all_to_all x1, blocking collectives, family_body(): arrived = lax.all_to_all(packed, ('brick', 'tile'), 0, 0, tiled=True)  15.5 us
    ppermute x3, starting transfers between devices, family_body(): lax.ppermute(message, 'tile', [(t, t ^ delta) for t in range(tile_count)])  4.64 us
    ppermute x3, waiting for transfers between devices, family_body(): lax.ppermute(message, 'tile', [(t, t ^ delta) for t in range(tile_count)])  3.79 us
    ppermute x1, waiting for transfers between devices, family_body(): far = lax.ppermute(skin, ('brick', 'tile'), pairs)  1.88 us
    pallas_call x1, Pallas kernels, family_body(): pl.pallas_call(functools.partial(pack_kernel, group_len, dests), out_shap...  1.69 us
    pallas_call x1, Pallas kernels, family_body(): pl.pallas_call(functools.partial(turn_kernel, channels, CB_DEV * owners),...  1.49 us
    pallas_call x1, Pallas kernels, family_body(): pl.pallas_call(functools.partial(grid_kernel, channels), out_shape=(jax.S...  1.27 us
    pallas_call x1, Pallas kernels, family_body(): pl.pallas_call(functools.partial(combine_kernel, channels), out_shape=jax...  0.82 us
  transfers between devices with their start and end apart: 4, of which 3 were waited for; matrix products, arithmetic and copies ran while one was open for 0% of the time, Pallas kernels for 5%

profile of v2, /device:TPU:0, one launch (start us, length us, event | category | flops | bytes accessed | tf_op | source)
XLA Modules:
  0.0 32.4 jit_solution(4295200994835386896)
XLA Ops:
  0.6 1.7 %pack.1 = (bf16[32,16,128]{2,1,0:T(8,128)(2,1)S(1)}, bf16[4,256,256]{2,1,0:T(8,128)(2,1)S(1)}) custom-call(s32[8,128]{1,0:T(8,128)} %bitcast.9, s32[8,128]{1,0:T(8,128)} %bitcast.10, bf16[28,1024]{1,0:T(8,128)(2,1)} %grad_hbm.1, bf16[4,256,256]{2,1,0:T(8,128)(2,1)} %constant.4.clone.plane_hbm), custom_call_target="tpu_custom_call" | custom-call | tf_op jit(solution)/shard_map/pack/pallas_call | solution.py:539
  2.3 15.5 %all_to_all.5.arrived_ref = bf16[32,16,128]{2,1,0:T(8,128)(2,1)S(1)} all-to-all(bf16[32,16,128]{2,1,0:T(8,128)(2,1)S(1)} %get-tuple-element.9), channel_id=1, replica_groups=mesh['brick'=8,'tile'=4] {'brick','tile'}, dimensions={0} | all-to-all | bytes 262144 | tf_op jit(solution)/shard_map/all_to_all | solution.py:562
  17.8 1.3 %grid.1 = (f32[256,512]{1,0:T(8,128)S(1)}, f32[4,28,128]{2,1,0:T(8,128)S(1)}, f32[4,28,128]{2,1,0:T(8,128)S(1)}) custom-call(bf16[32,16,128]{2,1,0:T(8,128)(2,1)S(1)} %all_to_all.5.arrived_ref, bf16[4,256,256]{2,1,0:T(8,128)(2,1)S(1)} %get-tuple-element.10.plane_ref), custom_call_target="tpu_custom_call" | custom-call | tf_op jit(solution)/shard_map/grid/pallas_call | solution.py:564
  19.1 0.1 collective-permute-start
  19.2 1.9 %collective-permute-done.far_ref = f32[4,28,128]{2,1,0:T(8,128)S(1)} collective-permute-done((f32[4,28,128]{2,1,0:T(8,128)S(1)}, f32[4,28,128]{2,1,0:T(8,128)S(1)}, u32[]{:S(2)}, u32[]{:S(2)}) %collective-permute-start) | collective-permute-done | bytes 57376 | tf_op jit(solution)/shard_map/ppermute | solution.py:578
  21.1 0.7 %collective-permute-start.1 = (f32[3,28,128]{2,1,0:T(8,128)S(1)}, f32[3,28,128]{2,1,0:T(8,128)S(1)}, u32[]{:S(2)}, u32[]{:S(2)}) collective-permute-start(f32[3,28,128]{2,1,0:T(8,128)S(1)} %pad_maximum_fusion), channel_id=1, source_target_pairs={{0,1},{1,0},{2,3},{3,2},{4,5},{5,4},{6,7},{7,6},{8,9},{9,8},{10,11... | collective-permute-start | bytes 129032 | tf_op jit(solution)/shard_map/ppermute | solution.py:594
  21.8 3.8 %collective-permute-start.2 = (f32[3,28,128]{2,1,0:T(8,128)S(1)}, f32[3,28,128]{2,1,0:T(8,128)S(1)}, u32[]{:S(2)}, u32[]{:S(2)}) collective-permute-start(f32[3,28,128]{2,1,0:T(8,128)S(1)} %pad_maximum_fusion.1), channel_id=1, source_target_pairs={{0,2},{1,3},{2,0},{3,1},{4,6},{5,7},{6,4},{7,5},{8,10},{9,11},{10,... | collective-permute-start | bytes 129032 | tf_op jit(solution)/shard_map/ppermute | solution.py:594
  25.6 0.0 copy-start.1
  25.6 0.1 collective-permute-start.3
  25.8 0.5 %copy-done.1 = s32[4,6]{1,0:T(4,128)S(1)} copy-done((s32[4,6]{1,0:T(4,128)S(1)}, s32[4,6]{1,0:T(4,128)}, u32[]{:S(2)}) %copy-start.1) | copy-done | bytes 120
  26.3 0.0 copy-start
  26.3 1.5 %turn.1 = (f32[224,512]{1,0:T(8,128)}, s32[4,8,128]{2,1,0:T(8,128)S(1)}) custom-call(f32[256,512]{1,0:T(8,128)S(1)} %get-tuple-element.11.rows_ref, s32[4,6]{1,0:T(4,128)S(1)} %copy-done.1), custom_call_target="tpu_custom_call" | custom-call | tf_op jit(solution)/shard_map/turn/pallas_call | solution.py:579
  27.8 0.0 collective-permute-done.1.one_ref
  27.8 1.8 %collective-permute-done.2.two_ref = f32[3,28,128]{2,1,0:T(8,128)S(1)} collective-permute-done((f32[3,28,128]{2,1,0:T(8,128)S(1)}, f32[3,28,128]{2,1,0:T(8,128)S(1)}, u32[]{:S(2)}, u32[]{:S(2)}) %collective-permute-start.2) | collective-permute-done | bytes 43040 | tf_op jit(solution)/shard_map/ppermute | solution.py:594
  29.6 2.0 %collective-permute-done.3.three_ref = f32[3,28,128]{2,1,0:T(8,128)S(1)} collective-permute-done((f32[3,28,128]{2,1,0:T(8,128)S(1)}, f32[3,28,128]{2,1,0:T(8,128)S(1)}, u32[]{:S(2)}, u32[]{:S(2)}) %collective-permute-start.3) | collective-permute-done | bytes 43040 | tf_op jit(solution)/shard_map/ppermute | solution.py:594
  31.6 0.0 copy-done
  31.6 0.8 %combine.1 = f32[112,128]{1,0:T(8,128)} custom-call(s32[4,8,128]{2,1,0:T(8,128)S(1)} %get-tuple-element.13.source_ref, f32[4,28,128]{2,1,0:T(8,128)S(1)} %get-tuple-element.14.own_ref, f32[4,28,128]{2,1,0:T(8,128)S(1)} %get-tuple-element.15.skin_ref, f32[4,28,128]{2,1,0:T(8,128)S(1)} %collective-permute-done.far_ref, ...), custom_call_target="tpu_custom_call" | custom-call | tf_op jit(solution)/shard_map/combine/pallas_call | solution.py:595
  (5 shorter events, 0.0 us)
Async XLA Ops:
  19.1 2.0 %collective-permute-start = (f32[4,28,128]{2,1,0:T(8,128)S(1)}, f32[4,28,128]{2,1,0:T(8,128)S(1)}, u32[]{:S(2)}, u32[]{:S(2)}) collective-permute-start(f32[4,28,128]{2,1,0:T(8,128)S(1)} %get-tuple-element.15.skin_ref), channel_id=1, source_target_pairs={{0,28},{1,29},{2,6},{3,7},{4,0},{5,1},{6,10},{7,11},{8,4},{9,5},{1... | collective-permute-start | bytes 172040 | tf_op jit(solution)/shard_map/ppermute | solution.py:578
  21.1 6.7 %collective-permute-start.1 = (f32[3,28,128]{2,1,0:T(8,128)S(1)}, f32[3,28,128]{2,1,0:T(8,128)S(1)}, u32[]{:S(2)}, u32[]{:S(2)}) collective-permute-start(f32[3,28,128]{2,1,0:T(8,128)S(1)} %pad_maximum_fusion), channel_id=1, source_target_pairs={{0,1},{1,0},{2,3},{3,2},{4,5},{5,4},{6,7},{7,6},{8,9},{9,8},{10,11... | collective-permute-start | bytes 129032 | tf_op jit(solution)/shard_map/ppermute | solution.py:594
  21.8 7.7 %collective-permute-start.2 = (f32[3,28,128]{2,1,0:T(8,128)S(1)}, f32[3,28,128]{2,1,0:T(8,128)S(1)}, u32[]{:S(2)}, u32[]{:S(2)}) collective-permute-start(f32[3,28,128]{2,1,0:T(8,128)S(1)} %pad_maximum_fusion.1), channel_id=1, source_target_pairs={{0,2},{1,3},{2,0},{3,1},{4,6},{5,7},{6,4},{7,5},{8,10},{9,11},{10,... | collective-permute-start | bytes 129032 | tf_op jit(solution)/shard_map/ppermute | solution.py:594
  25.6 0.7 %copy-start.1 = (s32[4,6]{1,0:T(4,128)S(1)}, s32[4,6]{1,0:T(4,128)}, u32[]{:S(2)}) copy-start(s32[4,6]{1,0:T(4,128)} %near_ref.1) | copy-start | bytes 292
  25.6 6.0 %collective-permute-start.3 = (f32[3,28,128]{2,1,0:T(8,128)S(1)}, f32[3,28,128]{2,1,0:T(8,128)S(1)}, u32[]{:S(2)}, u32[]{:S(2)}) collective-permute-start(f32[3,28,128]{2,1,0:T(8,128)S(1)} %pad_maximum_fusion.2), channel_id=1, source_target_pairs={{0,3},{1,2},{2,1},{3,0},{4,7},{5,6},{6,5},{7,4},{8,11},{9,10},{10,... | collective-permute-start | bytes 129032 | tf_op jit(solution)/shard_map/ppermute | solution.py:594
  26.3 5.3 %copy-start = (bf16[2,128,128]{2,1,0:T(8,128)(2,1)S(1)}, bf16[2,128,128]{2,1,0:T(8,128)(2,1)}, u32[]{:S(2)}) copy-start(bf16[2,128,128]{2,1,0:T(8,128)(2,1)} %constant.5.clone.table_ref) | copy-start | bytes 196612

commit v3 on v2

--- a/solution.py
+++ b/solution.py
@@ -246,45 +246,6 @@
 KERNEL_VMEM = 16 * 1024 * 1024
 
 
-def plane_weights(brick_edge):
-    table = np.zeros((2, brick_edge, brick_edge + 2), np.float32)
-    for half in range(2):
-        for cell in range(brick_edge):
-            at = half * brick_edge + cell
-            table[half, cell, at // 2 + 1] += 0.75
-            table[half, cell, at // 2 - 1 + 2 * (at % 2) + 1] += 0.25
-    return table
-
-
-def plane_matrices(brick_edge):
-    weight = plane_weights(brick_edge)
-    square = brick_edge * brick_edge
-    full = np.einsum("aym,bzn->abyzmn", weight, weight).reshape(4 * square, brick_edge + 2, brick_edge + 2)
-    out = np.zeros((4, 4 * square, 2 * LANES), np.float32)
-    last = brick_edge - 1
-    for m2 in range(-1, brick_edge + 1):
-        for m3 in range(-1, brick_edge + 1):
-            column = full[:, m2 + 1, m3 + 1]
-            out_y = m2 < 0 or m2 > last
-            out_z = m3 < 0 or m3 > last
-            cell = min(max(m2, 0), last) * brick_edge + min(max(m3, 0), last)
-            for odd in range(2):
-                if out_y == out_z:
-                    out[odd, :, odd * square + cell] += column
-                elif out_y:
-                    face = 0 if m2 < 0 else 1
-                    out[odd, :, LANES + (odd * 4 + face) * brick_edge + m3] += column
-                else:
-                    face = 2 if m3 < 0 else 3
-                    out[odd, :, LANES + (odd * 4 + face) * brick_edge + m2] += column
-            for side in range(2):
-                if out_y or out_z:
-                    out[2 + side, :, side * square + cell] += column
-                else:
-                    out[2 + side, :, LANES + square + cell] += column
-    return out
-
-
 def expand_tables(brick_edge):
     square = brick_edge * brick_edge
     last = brick_edge - 1
@@ -312,15 +273,14 @@
     return lax.dot_general(left, right, (((1,), (1,)), ((), ())), preferred_element_type=jnp.float32)
 
 
-def pack_kernel(group_len, dests, brick_hbm, slot_hbm, grad_hbm, plane_hbm, out_ref, plane_ref, brick_ref, slot_ref, grad_ref, high_ref, sems):
+def pack_kernel(group_len, partners, brick_hbm, slot_hbm, grad_hbm, out_ref, brick_ref, slot_ref, grad_ref, high_ref, sems):
     channels = grad_hbm.shape[0]
     blocks = brick_ref.shape[0]
-    square = E * E
+    dests = len(partners)
     copies = [
         pltpu.make_async_copy(brick_hbm, brick_ref, sems.at[0]),
         pltpu.make_async_copy(slot_hbm, slot_ref, sems.at[1]),
         pltpu.make_async_copy(grad_hbm, grad_ref, sems.at[2]),
-        pltpu.make_async_copy(plane_hbm, plane_ref, sems.at[3]),
     ]
     for copy in copies:
         copy.start()
@@ -333,8 +293,9 @@
     slot = slot_ref[...]
     bucket = brick // group_len
     local = brick - bucket * group_len
-    plane = slot // square
-    cell = slot - plane * square
+    coord_x = (local // 4) * E + slot // (E * E)
+    coord_y = (local // 2 % 2) * E + slot // E % E
+    coord_z = (local % 2) * E + slot % E
     bucket_f = bucket.astype(jnp.float32)
     dest_ids = lax.broadcasted_iota(jnp.int32, (dests, LANES), 0).astype(jnp.float32)
     hots = [
@@ -353,14 +314,14 @@
     rank = jnp.concatenate(ranks, axis=1)
 
     rows = lax.broadcasted_iota(jnp.int32, (4, LANES), 0)
-    local_f = (local + 1).astype(jnp.float32)
-    plane_f = plane.astype(jnp.float32)
-    cell_f = cell.astype(jnp.float32)
+    x_f = coord_x.astype(jnp.float32)
+    y_f = coord_y.astype(jnp.float32)
+    z_f = coord_z.astype(jnp.float32)
     for i in range(blocks):
         code = jnp.where(
             rows == 0,
-            local_f[i : i + 1],
-            jnp.where(rows == 1, plane_f[i : i + 1], jnp.where(rows == 2, cell_f[i : i + 1], 0.0)),
+            x_f[i : i + 1],
+            jnp.where(rows == 1, y_f[i : i + 1], jnp.where(rows == 2, z_f[i : i + 1], 0.0)),
         )
         high_ref[channels - 16 : channels - 12, i * LANES : (i + 1) * LANES] = code.astype(jnp.bfloat16)
     copies[2].wait()
@@ -383,106 +344,121 @@
     hot_high = jnp.where(rank_ids == rank + half, 1.0, 0.0).astype(jnp.bfloat16)
     placed = contract_last(jnp.concatenate(low_rows, axis=0), hot_low)
     placed = placed + contract_last(jnp.concatenate(high_rows, axis=0), hot_high)
-    out_ref[...] = placed.astype(jnp.bfloat16).reshape(dests, 16, LANES)
-    copies[3].wait()
-
-
-def grid_kernel(channels, arrived_ref, plane_ref, fine_ref, own_ref, skin_ref, quarter_ref):
-    tile_id = lax.axis_index("tile")
-    sources = arrived_ref.shape[0]
+    placed = placed.astype(jnp.bfloat16).reshape(dests, 16, LANES)
+    for dest in range(dests):
+        out_ref[dest, 0] = placed[dest]
+        out_ref[dest, 1] = placed[partners[dest]]
+
+
+def unpack(arrived_ref, which, channels):
     half = LANES // 2
+    pairs = arrived_ref.shape[0] // 2
     lows = []
     highs = []
-    for p in range(sources // 2):
-        first = arrived_ref[p]
-        second = arrived_ref[p + sources // 2]
+    for p in range(pairs):
+        first = arrived_ref[p, which]
+        second = arrived_ref[p + pairs, which]
         lows.append(jnp.concatenate([first[:, :half], second[:, :half]], axis=1))
         highs.append(jnp.concatenate([first[:, half:], second[:, half:]], axis=1))
     low = jnp.concatenate(lows, axis=1)
     high = jnp.concatenate(highs, axis=1)
-    total = low.shape[1]
     codes = high.astype(jnp.float32)
     at = channels - 16
-    brick16 = jnp.broadcast_to(codes[at : at + 1], (16, total)).astype(jnp.bfloat16)
-    plane16 = jnp.broadcast_to(codes[at + 1 : at + 2], (16, total)).astype(jnp.bfloat16)
-    cell16 = jnp.broadcast_to(codes[at + 2 : at + 3], (16, total)).astype(jnp.bfloat16)
-    zero = jnp.zeros_like(low)
-    one = jnp.ones_like(low)
-    left = []
-    for child in range(8):
-        mask = brick16 == jnp.bfloat16(child + 1)
-        left.append(jnp.where(mask, low, zero))
-        left.append(jnp.where(mask, high, zero))
-    row_ids = lax.broadcasted_iota(jnp.int32, (16, total), 0).astype(jnp.float32)
-    cells = [
-        jnp.where(cell16 == (row_ids + 16.0 * g).astype(jnp.bfloat16), one, zero) for g in range(E * E // 16)
+    coords = [
+        jnp.broadcast_to(codes[at + k : at + k + 1], (16, low.shape[1])).astype(jnp.bfloat16) for k in range(3)
     ]
-    right = []
-    for plane in range(E):
-        mask = plane16 == jnp.bfloat16(plane)
-        for g in range(E * E // 16):
-            right.append(jnp.where(mask, cells[g], zero))
-    fine = contract_last(jnp.concatenate(left, axis=0), jnp.concatenate(right, axis=0))
-    parts = [fine[32 * child : 32 * child + 32] for child in range(8)]
-    fine_ref[...] = fine
-
-    lane = lax.broadcasted_iota(jnp.int32, (32, LANES), 1)
-    first_half = lane < half
-    blank = jnp.zeros((32, LANES), jnp.float32)
-
-    def slab(child, m):
-        return parts[child][:, m * LANES : (m + 1) * LANES] if 0 <= m < E // 2 else blank
-
-    def along_x(child, m):
-        value = 0.25 * jnp.where(first_half, slab(child, m + 1), slab(child, m - 1))
-        return value + 0.75 * slab(child, m) if 0 <= m < E // 2 else value
-
-    def layer(m):
-        columns = []
-        for kyz in range(4):
-            if m <= E // 2 and m >= E // 2 - 1:
-                columns.append(along_x(kyz, m) + along_x(4 + kyz, m - E // 2))
-            elif m < E // 2:
-                columns.append(along_x(kyz, m))
-            else:
-                columns.append(along_x(4 + kyz, m - E // 2))
-        return jnp.concatenate(columns, axis=1)
-
-    def matrix(which):
-        pieces = []
-        for kyz in range(4):
-            piece = plane_ref[which, kyz * half : (kyz + 1) * half, :]
-            pieces += [piece, piece]
-        return jnp.concatenate(pieces, axis=0)
-
-    def apply(stack, table):
-        high_part, low_part = split_two(stack)
-        return jnp.dot(high_part, table, preferred_element_type=jnp.float32) + jnp.dot(
-            low_part, table, preferred_element_type=jnp.float32
-        )
-
-    even = jnp.concatenate([layer(2 * q) for q in range(4)], axis=0)
-    odd = jnp.concatenate([layer(2 * q + 1) for q in range(4)], axis=0)
-    inner = apply(even, matrix(0)) + apply(odd, matrix(1))
-    below = apply(layer(-1), matrix(2))
-    above = apply(layer(E), matrix(3))
-    for q in range(4):
-        own = inner[32 * q : 32 * q + 32, :LANES]
-        skin = inner[32 * q : 32 * q + 32, LANES:]
-        if q == 0:
-            own = own + below[:, :LANES]
-            skin = skin + above[:, LANES:]
-        if q == 3:
-            own = own + above[:, :LANES]
-            skin = skin + below[:, LANES:]
-        quarter_ref[q, 0] = own
-        quarter_ref[q, 1] = skin
+    return low, high, coords
+
+
+def tent(halved, cell):
+    return jnp.maximum(jnp.bfloat16(1.0) - jnp.abs(halved - (cell + jnp.bfloat16(0.25))), jnp.bfloat16(0.0))
+
+
+def sample_weights(coords, with_own):
+    x, y, z = coords
+    shape = x.shape
+    quarter = jnp.bfloat16(0.25)
+    half = jnp.bfloat16(0.5)
+    zero = jnp.zeros(shape, jnp.bfloat16)
+    last = 2 * E - 1
+    row = lax.broadcasted_iota(jnp.int32, shape, 0)
+    upper = row >= E
+    along = jnp.where(upper, row - E, row).astype(jnp.float32).astype(jnp.bfloat16)
+    upper_f = jnp.where(upper, 1.0, 0.0).astype(jnp.bfloat16)
+    ends = upper_f * jnp.bfloat16(last)
+    x_half, y_half, z_half = x * half, y * half, z * half
+    z_in = tent(z_half, along)
+    y_in = tent(y_half, along)
+    y_pair = [tent(y_half, upper_f + jnp.bfloat16(2 * g)) for g in range(E // 2)]
+    x_in = [tent(x_half, jnp.bfloat16(m)) for m in range(E)]
+    x_low = jnp.where(x == jnp.bfloat16(0), quarter, zero)
+    x_high = jnp.where(x == jnp.bfloat16(last), quarter, zero)
+    plane = [y_pair[g] * z_in for g in range(E // 2)]
+    own = []
+    if with_own:
+        far = jnp.bfloat16(-1)
+        z_ends = jnp.where(along == jnp.bfloat16(0), jnp.bfloat16(0), far)
+        z_ends = jnp.where(along == jnp.bfloat16(E - 1), jnp.bfloat16(last), z_ends)
+        z_out = jnp.where(z == z_ends, quarter, zero)
+        y_first = jnp.where(y == jnp.where(upper_f == jnp.bfloat16(0), jnp.bfloat16(0), far), quarter, zero)
+        y_last = jnp.where(y == jnp.where(upper_f == jnp.bfloat16(1), jnp.bfloat16(last), far), quarter, zero)
+        z_both = z_in + z_out
+        inner = list(plane)
+        outer = [y_pair[g] * z_out for g in range(E // 2)]
+        for g, y_out in ((0, y_first), (E // 2 - 1, y_last)):
+            inner[g] = inner[g] + y_out * z_out
+            outer[g] = outer[g] + y_out * z_both
+        for m in range(E):
+            for g in range(E // 2):
+                value = x_in[m] * inner[g]
+                if m == 0:
+                    value = value + x_low * outer[g]
+                if m == E - 1:
+                    value = value + x_high * outer[g]
+                own.append(value)
+    y_face = jnp.where(y == ends, quarter, zero) * z_in
+    z_face = jnp.where(z == ends, quarter, zero) * y_in
+    skins = []
+    for m in range(E):
+        skins += [x_in[m] * y_face, x_in[m] * z_face]
+    skins += [x_low * plane[g] for g in range(E // 2)]
+    skins += [x_high * plane[g] for g in range(E // 2)]
+    return own, skins
+
+
+def skin_quarters(skins):
+    half = LANES // 2
+    lane = lax.broadcasted_iota(jnp.int32, (skins.shape[0], LANES), 1)
+    left = lane < half
+    parts = [skins[:, i * LANES : (i + 1) * LANES] for i in range(3)]
+    turned = [jnp.concatenate([part[:, half:], part[:, :half]], axis=1) for part in parts]
+    return [
+        jnp.where(left, parts[0], parts[2]),
+        jnp.where(left, turned[0], 0.0),
+        jnp.where(left, parts[1], 0.0),
+        jnp.where(left, turned[1], turned[2]),
+    ]
+
+
+def coarse_kernel(channels, arrived_ref, *refs):
+    out_refs, quarter_ref = refs[:4], refs[4]
+    tile_id = lax.axis_index("tile")
+    for which in range(2):
+        low, high, coords = unpack(arrived_ref, which, channels)
+        values = jnp.concatenate([low, high], axis=0)
+        own, skins = sample_weights(coords, which == 0)
+        product = contract_last(values, jnp.concatenate(own + skins, axis=0))
+        base = 16 * len(own)
+        for q, skin in enumerate(skin_quarters(product[:, base:])):
+            if which == 0:
+                quarter_ref[q, 0] = product[:, q * LANES : (q + 1) * LANES]
+            quarter_ref[q, 1 + which] = skin
     for delta in range(4):
-        own_ref[delta] = quarter_ref[tile_id ^ delta, 0][:channels]
-        skin_ref[delta] = quarter_ref[tile_id ^ delta, 1][:channels]
-
-
-def turn_kernel(channels, coarse_total, rows_ref, near_ref, fine_ref, source_ref, turn_ref):
+        for part in range(3):
+            out_refs[delta][part] = quarter_ref[tile_id ^ delta, part][:channels]
+
+
+def fine_kernel(channels, coarse_total, arrived_ref, near_ref, fine_ref, source_ref, turn_ref):
     first = lax.axis_index("brick") * CB_DEV - CB_DEV // 2
     lane = lax.broadcasted_iota(jnp.int32, (8, LANES), 1)
     group = jnp.where(lane < LANES // 2, (lane // E) % 4, 4)
@@ -493,21 +469,41 @@
         for k in range(2, 5):
             source = jnp.where(group == k, near[k], source)
         source_ref[i] = source
+    low, high, coords = unpack(arrived_ref, 0, channels)
+    zero = jnp.zeros_like(low)
+    one = jnp.ones_like(low)
+    edge = jnp.bfloat16(E)
+    halves = [jnp.where(c >= edge, one, zero) for c in coords]
+    inside = [c - edge * h for c, h in zip(coords, halves)]
+    child_at = halves[0] * jnp.bfloat16(4) + halves[1] * jnp.bfloat16(2) + halves[2]
+    cell_at = inside[1] * edge + inside[2]
+    left = []
+    for child in range(8):
+        mask = child_at == jnp.bfloat16(child)
+        left.append(jnp.where(mask, low, zero))
+        left.append(jnp.where(mask, high, zero))
+    row_ids = lax.broadcasted_iota(jnp.int32, low.shape, 0).astype(jnp.float32)
+    cells = [
+        jnp.where(cell_at == (row_ids + 16.0 * g).astype(jnp.bfloat16), one, zero) for g in range(E * E // 16)
+    ]
+    right = []
+    for plane in range(E):
+        mask = inside[0] == jnp.bfloat16(plane)
+        for g in range(E * E // 16):
+            right.append(jnp.where(mask, cells[g], zero))
+    fine = contract_last(jnp.concatenate(left, axis=0), jnp.concatenate(right, axis=0))
     for i in range(V // LANES):
         for child in range(8):
-            turn_ref[i, pl.ds(child, channels, stride=8), :] = rows_ref[
+            turn_ref[i, pl.ds(child, channels, stride=8), :] = fine[
                 32 * child : 32 * child + channels, i * LANES : (i + 1) * LANES
             ]
         fine_ref[:, i * LANES : (i + 1) * LANES] = turn_ref[i]
 
 
-def combine_kernel(channels, source_ref, own_ref, skin_ref, far_ref, one_ref, two_ref, three_ref,
+def combine_kernel(channels, source_ref, zero_ref, one_ref, two_ref, three_ref,
                    table_ref, out_ref, hold_ref):
     tile_id = lax.axis_index("tile")
-    hold_ref[tile_id, 0] = own_ref[0]
-    hold_ref[tile_id, 1] = skin_ref[0]
-    hold_ref[tile_id, 2] = far_ref[0]
-    for delta, ref in ((1, one_ref), (2, two_ref), (3, three_ref)):
+    for delta, ref in enumerate((zero_ref, one_ref, two_ref, three_ref)):
         hold_ref[tile_id ^ delta] = ref[...]
     skins = [hold_ref[2, 2], hold_ref[3, 2]]
     skins += [hold_ref[j, 1] for j in range(4)]
@@ -536,48 +532,49 @@
     dests = owners * tile_count
     group_len = FB_DEV // tile_count
     vmem = pl.BlockSpec(memory_space=pltpu.VMEM)
-    packed, planes = pl.pallas_call(
-        functools.partial(pack_kernel, group_len, dests),
-        out_shape=(
-            jax.ShapeDtypeStruct((dests, 16, LANES), jnp.bfloat16),
-            jax.ShapeDtypeStruct((4, 4 * E * E, 2 * LANES), jnp.bfloat16),
-        ),
-        in_specs=[pl.BlockSpec(memory_space=pltpu.HBM)] * 4,
-        out_specs=(vmem, vmem),
+    hbm = pl.BlockSpec(memory_space=pltpu.HBM)
+    limit = pltpu.CompilerParams(vmem_limit_bytes=KERNEL_VMEM)
+    partners = []
+    for b in range(owners):
+        for t in range(tile_count):
+            step = -1 if t >= tile_count // 2 else 1
+            partners.append((b + step) % owners * tile_count + t)
+    inputs = (
+        sample_brick.reshape(samples // LANES, LANES),
+        sample_slot.reshape(samples // LANES, LANES),
+        sample_grad,
+    )
+    packed = pl.pallas_call(
+        functools.partial(pack_kernel, group_len, tuple(partners)),
+        out_shape=jax.ShapeDtypeStruct((dests, 2, 16, LANES), jnp.bfloat16),
+        in_specs=[hbm] * 3,
+        out_specs=vmem,
         scratch_shapes=[
             pltpu.VMEM((samples // LANES, LANES), jnp.int32),
             pltpu.VMEM((samples // LANES, LANES), jnp.int32),
             pltpu.VMEM((channels, samples), jnp.bfloat16),
             pltpu.VMEM((16, samples), jnp.bfloat16),
-            pltpu.SemaphoreType.DMA((4,)),
+            pltpu.SemaphoreType.DMA((3,)),
         ],
-        compiler_params=pltpu.CompilerParams(vmem_limit_bytes=KERNEL_VMEM),
+        compiler_params=limit,
         name="pack",
-    )(
-        pltpu.with_memory_space_constraint(sample_brick.reshape(samples // LANES, LANES), pltpu.HBM),
-        pltpu.with_memory_space_constraint(sample_slot.reshape(samples // LANES, LANES), pltpu.HBM),
-        pltpu.with_memory_space_constraint(sample_grad, pltpu.HBM),
-        pltpu.with_memory_space_constraint(jnp.asarray(plane_matrices(E), jnp.bfloat16), pltpu.HBM),
-    )
+    )(*[pltpu.with_memory_space_constraint(value, pltpu.HBM) for value in inputs])
     arrived = lax.all_to_all(packed, ("brick", "tile"), 0, 0, tiled=True)
-    quarter = jax.ShapeDtypeStruct((4, channels, LANES), jnp.float32)
-    rows, own, skin = pl.pallas_call(
-        functools.partial(grid_kernel, channels),
-        out_shape=(jax.ShapeDtypeStruct((8 * 32, V), jnp.float32), quarter, quarter),
-        in_specs=[vmem, vmem],
-        out_specs=(vmem,) * 3,
-        scratch_shapes=[pltpu.VMEM((4, 2, 32, LANES), jnp.float32)],
-        compiler_params=pltpu.CompilerParams(vmem_limit_bytes=KERNEL_VMEM),
-        name="grid",
-    )(arrived, planes)
-    pairs = []
-    for b in range(owners):
-        for t in range(tile_count):
-            step = 1 if t >= tile_count // 2 else -1
-            pairs.append((b * tile_count + t, (b + step) % owners * tile_count + t))
-    far = lax.ppermute(skin, ("brick", "tile"), pairs)
+    message = jax.ShapeDtypeStruct((3, channels, LANES), jnp.float32)
+    messages = pl.pallas_call(
+        functools.partial(coarse_kernel, channels),
+        out_shape=(message,) * 4,
+        in_specs=[vmem],
+        out_specs=(vmem,) * 4,
+        scratch_shapes=[pltpu.VMEM((4, 3, 32, LANES), jnp.float32)],
+        compiler_params=limit,
+        name="coarse",
+    )(arrived)
+    arrivals = {}
+    for delta in (3, 1, 2):
+        arrivals[delta] = lax.ppermute(messages[delta], "tile", [(t, t ^ delta) for t in range(tile_count)])
     fine, source = pl.pallas_call(
-        functools.partial(turn_kernel, channels, CB_DEV * owners),
+        functools.partial(fine_kernel, channels, CB_DEV * owners),
         out_shape=(
             jax.ShapeDtypeStruct((channels * 8, V), jnp.float32),
             jax.ShapeDtypeStruct((CB_DEV, 8, LANES), jnp.int32),
@@ -585,22 +582,18 @@
         in_specs=[vmem, pl.BlockSpec(memory_space=pltpu.SMEM)],
         out_specs=(vmem, vmem),
         scratch_shapes=[pltpu.VMEM((V // LANES, channels * 8, LANES), jnp.float32)],
-        compiler_params=pltpu.CompilerParams(vmem_limit_bytes=KERNEL_VMEM),
-        name="turn",
-    )(rows, neighbour)
-    arrivals = {}
-    for delta in (3, 2, 1):
-        message = jnp.stack([own[delta], skin[delta], far[delta]])
-        arrivals[delta] = lax.ppermute(message, "tile", [(t, t ^ delta) for t in range(tile_count)])
+        compiler_params=limit,
+        name="fine",
+    )(arrived, neighbour)
     coarse = pl.pallas_call(
         functools.partial(combine_kernel, channels),
         out_shape=jax.ShapeDtypeStruct((channels * CB_DEV, LANES), jnp.float32),
-        in_specs=[vmem] * 8,
+        in_specs=[vmem] * 6,
         out_specs=vmem,
         scratch_shapes=[pltpu.VMEM((4, 3, channels, LANES), jnp.float32)],
-        compiler_params=pltpu.CompilerParams(vmem_limit_bytes=KERNEL_VMEM),
+        compiler_params=limit,
         name="combine",
-    )(source, own, skin, far, arrivals[1], arrivals[2], arrivals[3], jnp.asarray(expand_tables(E), jnp.bfloat16))
+    )(source, messages[0], arrivals[1], arrivals[2], arrivals[3], jnp.asarray(expand_tables(E), jnp.bfloat16))
     fine_grad = fine.reshape(channels, 8, V).transpose(1, 0, 2)
     coarse_grad = coarse.reshape(channels, CB_DEV, LANES).transpose(1, 0, 2)
     return fine_grad, coarse_grad

time: 32.6 us -> 30.9 us (0.948)
  waiting for transfers between devices: 5.67 us -> 1.59 us
  blocking collectives: 15.5 us -> 17.4 us
  Pallas kernels: 5.28 us -> 6.57 us
  local copies, waits for them, and re-layouts: 0.56 us -> 0.01 us
    ppermute x4 -> x3, waiting for transfers between devices: 5.67 us -> 1.59 us  [family_body(): lax.ppermute(messages[delta], 'tile', [(t, t ^ delta) for t in range(tile...]
    all_to_all x1, blocking collectives: 15.5 us -> 17.4 us  [family_body(): arrived = lax.all_to_all(packed, ('brick', 'tile'), 0, 0, tiled=True)]
    pallas_call x3, Pallas kernels: 4.45 us -> 5.74 us  [the longest x1 2.26 us: family_body(): pl.pallas_call(functools.partial(fine_kernel, channels, CB_DEV * owners),...]
    unnamed x4, local copies, waits for them, and re-layouts: 0.55 us -> 0.01 us
    ppermute x4 -> x3, starting transfers between devices: 4.69 us -> 4.45 us  [family_body(): lax.ppermute(messages[delta], 'tile', [(t, t ^ delta) for t in range(tile...]
  transfers between devices with their start and end apart: 4 -> 3, of which waited for: 3 -> 2; matrix products, arithmetic and copies ran while one was open for 0% -> 0% of each run, Pallas kernels for 5% -> 7%
where the time goes in v3:
time: 30.9 us; the launch traced here: 30.6 us
  blocking collectives  17.4 us (56%)
  Pallas kernels  6.57 us (21%)
  starting transfers between devices  4.45 us (14%)
  waiting for transfers between devices  1.59 us (5%)
  between operations  0.66 us (2%)
    all_to_all x1, blocking collectives, family_body(): arrived = lax.all_to_all(packed, ('brick', 'tile'), 0, 0, tiled=True)  17.4 us
    ppermute x3, starting transfers between devices, family_body(): lax.ppermute(messages[delta], 'tile', [(t, t ^ delta) for t in range(tile...  4.45 us
    pallas_call x1, Pallas kernels, family_body(): pl.pallas_call(functools.partial(fine_kernel, channels, CB_DEV * owners),...  2.26 us
    pallas_call x1, Pallas kernels, family_body(): pl.pallas_call(functools.partial(coarse_kernel, channels), out_shape=(mes...  1.81 us
    pallas_call x1, Pallas kernels, family_body(): pl.pallas_call(functools.partial(pack_kernel, group_len, tuple(partners))...  1.68 us
    ppermute x3, waiting for transfers between devices, family_body(): lax.ppermute(messages[delta], 'tile', [(t, t ^ delta) for t in range(tile...  1.59 us
    pallas_call x1, Pallas kernels, family_body(): pl.pallas_call(functools.partial(combine_kernel, channels), out_shape=jax...  0.82 us
  transfers between devices with their start and end apart: 3, of which 2 were waited for; matrix products, arithmetic and copies ran while one was open for 0% of the time, Pallas kernels for 7%

profile of v3, /device:TPU:0, one launch (start us, length us, event | category | flops | bytes accessed | tf_op | source)
XLA Modules:
  0.0 30.6 jit_solution(174272285940126312)
XLA Ops:
  0.6 1.7 %pack.1 = bf16[32,2,16,128]{3,2,1,0:T(8,128)(2,1)S(1)} custom-call(s32[8,128]{1,0:T(8,128)} %bitcast.9, s32[8,128]{1,0:T(8,128)} %bitcast.10, bf16[28,1024]{1,0:T(8,128)(2,1)} %grad_hbm.1), custom_call_target="tpu_custom_call" | custom-call | tf_op jit(solution)/shard_map/pack/pallas_call | solution.py:547
  2.3 17.4 %all_to_all.5.arrived_ref = bf16[32,2,16,128]{3,2,1,0:T(8,128)(2,1)S(1)} all-to-all(bf16[32,2,16,128]{3,2,1,0:T(8,128)(2,1)S(1)} %pack.1), channel_id=1, replica_groups=mesh['brick'=8,'tile'=4] {'brick','tile'}, dimensions={0} | all-to-all | bytes 524288 | tf_op jit(solution)/shard_map/all_to_all | solution.py:562
  19.7 1.8 %coarse.1 = (f32[3,28,128]{2,1,0:T(8,128)S(1)}, f32[3,28,128]{2,1,0:T(8,128)S(1)}, f32[3,28,128]{2,1,0:T(8,128)S(1)}, f32[3,28,128]{2,1,0:T(8,128)S(1)}) custom-call(bf16[32,2,16,128]{3,2,1,0:T(8,128)(2,1)S(1)} %all_to_all.5.arrived_ref), custom_call_target="tpu_custom_call" | custom-call | tf_op jit(solution)/shard_map/coarse/pallas_call | solution.py:564
  21.5 0.0 copy-start.1
  21.5 0.8 %collective-permute-start = (f32[3,28,128]{2,1,0:T(8,128)S(1)}, f32[3,28,128]{2,1,0:T(8,128)S(1)}, u32[]{:S(2)}, u32[]{:S(2)}) collective-permute-start(f32[3,28,128]{2,1,0:T(8,128)S(1)} %get-tuple-element.11), channel_id=1, source_target_pairs={{0,1},{1,0},{2,3},{3,2},{4,5},{5,4},{6,7},{7,6},{8,9},{9,8},{10,11... | collective-permute-start | bytes 129032 | tf_op jit(solution)/shard_map/ppermute | solution.py:575
  22.3 1.6 %collective-permute-start.1 = (f32[3,28,128]{2,1,0:T(8,128)S(1)}, f32[3,28,128]{2,1,0:T(8,128)S(1)}, u32[]{:S(2)}, u32[]{:S(2)}) collective-permute-start(f32[3,28,128]{2,1,0:T(8,128)S(1)} %get-tuple-element.12), channel_id=1, source_target_pairs={{0,2},{1,3},{2,0},{3,1},{4,6},{5,7},{6,4},{7,5},{8,10},{9,11},{10,... | collective-permute-start | bytes 129032 | tf_op jit(solution)/shard_map/ppermute | solution.py:575
  23.8 0.0 copy-start
  23.8 2.1 %collective-permute-start.2 = (f32[3,28,128]{2,1,0:T(8,128)S(1)}, f32[3,28,128]{2,1,0:T(8,128)S(1)}, u32[]{:S(2)}, u32[]{:S(2)}) collective-permute-start(f32[3,28,128]{2,1,0:T(8,128)S(1)} %get-tuple-element.13), channel_id=1, source_target_pairs={{0,3},{1,2},{2,1},{3,0},{4,7},{5,6},{6,5},{7,4},{8,11},{9,10},{10,... | collective-permute-start | bytes 129032 | tf_op jit(solution)/shard_map/ppermute | solution.py:575
  26.0 0.0 copy-done.1
  26.0 2.3 %fine.1 = (f32[224,512]{1,0:T(8,128)}, s32[4,8,128]{2,1,0:T(8,128)S(1)}) custom-call(bf16[32,2,16,128]{3,2,1,0:T(8,128)(2,1)S(1)} %all_to_all.5.arrived_ref, s32[4,6]{1,0:T(4,128)S(1)} %copy-done.1), custom_call_target="tpu_custom_call" | custom-call | tf_op jit(solution)/shard_map/fine/pallas_call | solution.py:576
  28.2 0.0 collective-permute-done.one_ref
  28.2 0.6 %collective-permute-done.1.two_ref = f32[3,28,128]{2,1,0:T(8,128)S(1)} collective-permute-done((f32[3,28,128]{2,1,0:T(8,128)S(1)}, f32[3,28,128]{2,1,0:T(8,128)S(1)}, u32[]{:S(2)}, u32[]{:S(2)}) %collective-permute-start.1) | collective-permute-done | bytes 43040 | tf_op jit(solution)/shard_map/ppermute | solution.py:575
  28.8 1.0 %collective-permute-done.2.three_ref = f32[3,28,128]{2,1,0:T(8,128)S(1)} collective-permute-done((f32[3,28,128]{2,1,0:T(8,128)S(1)}, f32[3,28,128]{2,1,0:T(8,128)S(1)}, u32[]{:S(2)}, u32[]{:S(2)}) %collective-permute-start.2) | collective-permute-done | bytes 43040 | tf_op jit(solution)/shard_map/ppermute | solution.py:575
  29.8 0.0 copy-done
  29.8 0.8 %combine.1 = f32[112,128]{1,0:T(8,128)} custom-call(s32[4,8,128]{2,1,0:T(8,128)S(1)} %get-tuple-element.9.source_ref, f32[3,28,128]{2,1,0:T(8,128)S(1)} %get-tuple-element.10.zero_ref, f32[3,28,128]{2,1,0:T(8,128)S(1)} %collective-permute-done.one_ref, f32[3,28,128]{2,1,0:T(8,128)S(1)} %collective-permute-done.1.two_ref, ...), custom_call_target="tpu_custom_call" | custom-call | tf_op jit(solution)/shard_map/combine/pallas_call | solution.py:588
Async XLA Ops:
  21.5 4.5 %copy-start.1 = (s32[4,6]{1,0:T(4,128)S(1)}, s32[4,6]{1,0:T(4,128)}, u32[]{:S(2)}) copy-start(s32[4,6]{1,0:T(4,128)} %near_ref.1) | copy-start | bytes 292
  21.5 6.7 %collective-permute-start = (f32[3,28,128]{2,1,0:T(8,128)S(1)}, f32[3,28,128]{2,1,0:T(8,128)S(1)}, u32[]{:S(2)}, u32[]{:S(2)}) collective-permute-start(f32[3,28,128]{2,1,0:T(8,128)S(1)} %get-tuple-element.11), channel_id=1, source_target_pairs={{0,1},{1,0},{2,3},{3,2},{4,5},{5,4},{6,7},{7,6},{8,9},{9,8},{10,11... | collective-permute-start | bytes 129032 | tf_op jit(solution)/shard_map/ppermute | solution.py:575
  22.3 6.6 %collective-permute-start.1 = (f32[3,28,128]{2,1,0:T(8,128)S(1)}, f32[3,28,128]{2,1,0:T(8,128)S(1)}, u32[]{:S(2)}, u32[]{:S(2)}) collective-permute-start(f32[3,28,128]{2,1,0:T(8,128)S(1)} %get-tuple-element.12), channel_id=1, source_target_pairs={{0,2},{1,3},{2,0},{3,1},{4,6},{5,7},{6,4},{7,5},{8,10},{9,11},{10,... | collective-permute-start | bytes 129032 | tf_op jit(solution)/shard_map/ppermute | solution.py:575
  23.8 6.0 %copy-start = (bf16[2,128,128]{2,1,0:T(8,128)(2,1)S(1)}, bf16[2,128,128]{2,1,0:T(8,128)(2,1)}, u32[]{:S(2)}) copy-start(bf16[2,128,128]{2,1,0:T(8,128)(2,1)} %constant.2.clone.table_ref) | copy-start | bytes 196612
  23.8 6.0 %collective-permute-start.2 = (f32[3,28,128]{2,1,0:T(8,128)S(1)}, f32[3,28,128]{2,1,0:T(8,128)S(1)}, u32[]{:S(2)}, u32[]{:S(2)}) collective-permute-start(f32[3,28,128]{2,1,0:T(8,128)S(1)} %get-tuple-element.13), channel_id=1, source_target_pairs={{0,3},{1,2},{2,1},{3,0},{4,7},{5,6},{6,5},{7,4},{8,11},{9,10},{10,... | collective-permute-start | bytes 129032 | tf_op jit(solution)/shard_map/ppermute | solution.py:575

commit v4 on v3

--- a/solution.py
+++ b/solution.py
@@ -253,11 +253,11 @@
     for side in range(2):
         for odd in range(2):
             for at in range(brick_edge):
-                base = odd * 4 * brick_edge + at
+                base = odd * brick_edge + at
                 out[side, base, odd * square + last * brick_edge + at] = 1
-                out[side, base + brick_edge, odd * square + at] = 1
-                out[side, base + 2 * brick_edge, odd * square + at * brick_edge + last] = 1
-                out[side, base + 3 * brick_edge, odd * square + at * brick_edge] = 1
+                out[side, base + 2 * brick_edge, odd * square + at] = 1
+                out[side, base + 4 * brick_edge, odd * square + at * brick_edge + last] = 1
+                out[side, base + 6 * brick_edge, odd * square + at * brick_edge] = 1
         for cell in range(square):
             out[side, square + cell, side * square + cell] = 1
     return out
@@ -273,7 +273,7 @@
     return lax.dot_general(left, right, (((1,), (1,)), ((), ())), preferred_element_type=jnp.float32)
 
 
-def pack_kernel(group_len, partners, brick_hbm, slot_hbm, grad_hbm, out_ref, brick_ref, slot_ref, grad_ref, high_ref, sems):
+def pack_kernel(group_len, tile_count, partners, brick_hbm, slot_hbm, grad_hbm, out_ref, brick_ref, slot_ref, grad_ref, high_ref, sems):
     channels = grad_hbm.shape[0]
     blocks = brick_ref.shape[0]
     dests = len(partners)
@@ -328,26 +328,41 @@
     high_ref[: channels - 16, :] = grad_ref[16:channels, :]
     low = grad_ref[:16, :]
     high = high_ref[...]
-    bucket16 = jnp.concatenate(
-        [jnp.broadcast_to(bucket_f[i : i + 1], (16, LANES)) for i in range(blocks)], axis=1
-    ).astype(jnp.bfloat16)
+
+    def spread(value):
+        return jnp.concatenate(
+            [jnp.broadcast_to(value[i : i + 1], (16, LANES)) for i in range(blocks)], axis=1
+        ).astype(jnp.bfloat16)
+
+    owner16 = spread((bucket // tile_count).astype(jnp.float32))
+    tile16 = spread((bucket % tile_count).astype(jnp.float32))
     zero = jnp.zeros_like(low)
-    low_rows = []
-    high_rows = []
+    left = []
+    for owner in range(dests // tile_count):
+        mask = owner16 == jnp.bfloat16(owner)
+        left += [jnp.where(mask, low, zero), jnp.where(mask, high, zero)]
+    half = LANES // 2
+    rank16 = jnp.broadcast_to(rank, (16, rank.shape[1])).astype(jnp.bfloat16)
+    row_ids = lax.broadcasted_iota(jnp.int32, rank16.shape, 0).astype(jnp.float32)
+    ones = jnp.ones_like(low)
+    hot = [
+        jnp.where(rank16 == (row_ids + 16.0 * g).astype(jnp.bfloat16), ones, zero) for g in range(half // 16)
+    ]
+    right = []
+    for tile in range(tile_count):
+        mask = tile16 == jnp.bfloat16(tile)
+        right += [jnp.where(mask, value, zero) for value in hot]
+    placed = contract_last(jnp.concatenate(left, axis=0), jnp.concatenate(right, axis=0)).astype(jnp.bfloat16)
+    tiles = []
+    for owner in range(dests // tile_count):
+        for pair in range(tile_count // 2):
+            low_part = placed[32 * owner : 32 * owner + 16, pair * LANES : (pair + 1) * LANES]
+            high_part = placed[32 * owner + 16 : 32 * owner + 32, pair * LANES : (pair + 1) * LANES]
+            tiles.append(jnp.concatenate([low_part[:, :half], high_part[:, :half]], axis=1))
+            tiles.append(jnp.concatenate([low_part[:, half:], high_part[:, half:]], axis=1))
     for dest in range(dests):
-        mask = bucket16 == jnp.bfloat16(dest)
-        low_rows.append(jnp.where(mask, low, zero))
-        high_rows.append(jnp.where(mask, high, zero))
-    rank_ids = lax.broadcasted_iota(jnp.int32, (LANES, rank.shape[1]), 0).astype(jnp.float32)
-    half = LANES // 2
-    hot_low = jnp.where(rank_ids == rank, 1.0, 0.0).astype(jnp.bfloat16)
-    hot_high = jnp.where(rank_ids == rank + half, 1.0, 0.0).astype(jnp.bfloat16)
-    placed = contract_last(jnp.concatenate(low_rows, axis=0), hot_low)
-    placed = placed + contract_last(jnp.concatenate(high_rows, axis=0), hot_high)
-    placed = placed.astype(jnp.bfloat16).reshape(dests, 16, LANES)
-    for dest in range(dests):
-        out_ref[dest, 0] = placed[dest]
-        out_ref[dest, 1] = placed[partners[dest]]
+        out_ref[dest, 0] = tiles[dest]
+        out_ref[dest, 1] = tiles[partners[dest]]
 
 
 def unpack(arrived_ref, which, channels):
@@ -370,89 +385,148 @@
     return low, high, coords
 
 
-def tent(halved, cell):
-    return jnp.maximum(jnp.bfloat16(1.0) - jnp.abs(halved - (cell + jnp.bfloat16(0.25))), jnp.bfloat16(0.0))
-
-
-def sample_weights(coords, with_own):
-    x, y, z = coords
-    shape = x.shape
-    quarter = jnp.bfloat16(0.25)
-    half = jnp.bfloat16(0.5)
-    zero = jnp.zeros(shape, jnp.bfloat16)
+def pack_pair(first, second):
+    return jnp.concatenate([first, second], axis=0).astype(jnp.bfloat16)
+
+
+def block_axes(code, axis_ref):
+    row = lax.broadcasted_iota(jnp.int32, (8, LANES), 0).astype(jnp.float32)
+    axis_ref[0] = code
+    coords = [axis_ref[0, pl.ds(at, 8, stride=0), :] for at in (4, 5, 6)]
+    rows = [jnp.maximum(1.0 - jnp.abs(c * 0.5 - (row + 0.25)), 0.0) for c in coords]
+    return row, coords, rows
+
+
+def paired(axis_ref, at, rows):
+    axis_ref[at] = rows
+    lines = [axis_ref[at, pl.ds(m, 8, stride=0), :] for m in range(E)]
+    return [pack_pair(lines[2 * g], lines[2 * g + 1]) for g in range(E // 2)]
+
+
+def select_rows(hits, low, high):
+    zero = jnp.zeros_like(low)
+    rows = []
+    for hit in hits:
+        rows += [jnp.where(hit, low, zero), jnp.where(hit, high, zero)]
+    return rows
+
+
+def own_block(code, axis_ref, low, high):
+    row, (x, y, z), (_, y_rows, z_rows) = block_axes(code, axis_ref)
+    last = 2.0 * E - 1.0
+    blank = jnp.zeros((8, LANES), jnp.float32)
+    y_pair = paired(axis_ref, 2, y_rows)
+    z_in = pack_pair(z_rows, z_rows)
+    y_low = jnp.where(y == 0.0, 0.25, 0.0)
+    y_high = jnp.where(y == last, 0.25, 0.0)
+    z_low = jnp.where(z == 0.0, 0.25, 0.0)
+    z_high = jnp.where(z == last, 0.25, 0.0)
+    z_out = jnp.where(row == 0.0, z_low, jnp.where(row == E - 1.0, z_high, blank))
+    z_out = pack_pair(z_out, z_out)
+    z_both = z_in + z_out
+    plane = [y_pair[g] * z_in for g in range(E // 2)]
+    inner = list(plane)
+    outer = [y_pair[g] * z_out for g in range(E // 2)]
+    for g, y_out in ((0, pack_pair(y_low, blank)), (E // 2 - 1, pack_pair(blank, y_high))):
+        inner[g] = inner[g] + y_out * z_out
+        outer[g] = outer[g] + y_out * z_both
+    faces = [y_low * z_rows, y_high * z_rows, z_low * y_rows, z_high * y_rows]
+    x16 = pack_pair(x, x)
+    left = select_rows([x16 == jnp.bfloat16(at) for at in range(2 * E)], low, high)
+    return left, inner + [pack_pair(face, blank) for face in faces], outer + plane
+
+
+def skin_block(code, axis_ref, low, high):
+    _, coords, (x_rows, y_rows, z_rows) = block_axes(code, axis_ref)
     last = 2 * E - 1
-    row = lax.broadcasted_iota(jnp.int32, shape, 0)
-    upper = row >= E
-    along = jnp.where(upper, row - E, row).astype(jnp.float32).astype(jnp.bfloat16)
-    upper_f = jnp.where(upper, 1.0, 0.0).astype(jnp.bfloat16)
-    ends = upper_f * jnp.bfloat16(last)
-    x_half, y_half, z_half = x * half, y * half, z * half
-    z_in = tent(z_half, along)
-    y_in = tent(y_half, along)
-    y_pair = [tent(y_half, upper_f + jnp.bfloat16(2 * g)) for g in range(E // 2)]
-    x_in = [tent(x_half, jnp.bfloat16(m)) for m in range(E)]
-    x_low = jnp.where(x == jnp.bfloat16(0), quarter, zero)
-    x_high = jnp.where(x == jnp.bfloat16(last), quarter, zero)
-    plane = [y_pair[g] * z_in for g in range(E // 2)]
-    own = []
-    if with_own:
-        far = jnp.bfloat16(-1)
-        z_ends = jnp.where(along == jnp.bfloat16(0), jnp.bfloat16(0), far)
-        z_ends = jnp.where(along == jnp.bfloat16(E - 1), jnp.bfloat16(last), z_ends)
-        z_out = jnp.where(z == z_ends, quarter, zero)
-        y_first = jnp.where(y == jnp.where(upper_f == jnp.bfloat16(0), jnp.bfloat16(0), far), quarter, zero)
-        y_last = jnp.where(y == jnp.where(upper_f == jnp.bfloat16(1), jnp.bfloat16(last), far), quarter, zero)
-        z_both = z_in + z_out
-        inner = list(plane)
-        outer = [y_pair[g] * z_out for g in range(E // 2)]
-        for g, y_out in ((0, y_first), (E // 2 - 1, y_last)):
-            inner[g] = inner[g] + y_out * z_out
-            outer[g] = outer[g] + y_out * z_both
-        for m in range(E):
-            for g in range(E // 2):
-                value = x_in[m] * inner[g]
-                if m == 0:
-                    value = value + x_low * outer[g]
-                if m == E - 1:
-                    value = value + x_high * outer[g]
-                own.append(value)
-    y_face = jnp.where(y == ends, quarter, zero) * z_in
-    z_face = jnp.where(z == ends, quarter, zero) * y_in
-    skins = []
+    x_pair = paired(axis_ref, 1, x_rows)
+    y_pair = paired(axis_ref, 2, y_rows)
+    z_in = pack_pair(z_rows, z_rows)
+    y_in = pack_pair(y_rows, y_rows)
+    x16, y16, z16 = [pack_pair(c, c) for c in coords]
+    hits = [c == jnp.bfloat16(end) for c in (y16, z16, x16) for end in (0, last)]
+    left = select_rows(hits, low, high)
+    right = [value * z_in for value in x_pair] + [value * y_in for value in x_pair]
+    return left, right + [value * z_in for value in y_pair]
+
+
+def lay_out(blocks):
+    return jnp.concatenate(
+        [jnp.concatenate([block[i] for block in blocks], axis=1) for i in range(len(blocks[0]))], axis=0
+    )
+
+
+def own_quarters(product, folds):
+    half = LANES // 2
+    lane = lax.broadcasted_iota(jnp.int32, (32, LANES), 1)
+    left = lane < half
+    at_x = [product[32 * at : 32 * at + 32] for at in range(2 * E)]
+    first, second = 0.25 * folds[:32], 0.25 * folds[32:]
+    layers = []
     for m in range(E):
-        skins += [x_in[m] * y_face, x_in[m] * z_face]
-    skins += [x_low * plane[g] for g in range(E // 2)]
-    skins += [x_high * plane[g] for g in range(E // 2)]
-    return own, skins
-
-
-def skin_quarters(skins):
+        value = 0.75 * (at_x[2 * m] + at_x[2 * m + 1])
+        if m == 0:
+            value = value + 0.25 * at_x[2] + jnp.where(left, first, 0.0)
+        elif m == E - 1:
+            value = value + 0.25 * at_x[2 * m - 1] + jnp.where(left, second, 0.0)
+        else:
+            value = value + 0.25 * (at_x[2 * m - 1] + at_x[2 * m + 2])
+        layers.append(value)
+    quarters = []
+    for q in range(E // 2):
+        even, odd = layers[2 * q], layers[2 * q + 1]
+        faces = pltpu.roll(even, half, 1) + pltpu.roll(jnp.where(left, 0.0, odd), half + E, 1)
+        beyond = second if q == 0 else first if q == E // 2 - 1 else jnp.zeros_like(even)
+        quarters.append((jnp.where(left, even, pltpu.roll(odd, half, 1)), jnp.where(left, faces, beyond)))
+    return quarters
+
+
+def skin_quarters(product):
     half = LANES // 2
-    lane = lax.broadcasted_iota(jnp.int32, (skins.shape[0], LANES), 1)
-    left = lane < half
-    parts = [skins[:, i * LANES : (i + 1) * LANES] for i in range(3)]
-    turned = [jnp.concatenate([part[:, half:], part[:, :half]], axis=1) for part in parts]
-    return [
-        jnp.where(left, parts[0], parts[2]),
-        jnp.where(left, turned[0], 0.0),
-        jnp.where(left, parts[1], 0.0),
-        jnp.where(left, turned[1], turned[2]),
-    ]
+    lane = lax.broadcasted_iota(jnp.int32, (32, LANES), 1)
+    sides = [0.25 * product[32 * f : 32 * f + 32, :LANES] for f in range(4)]
+    ends = []
+    for f in (4, 5):
+        end = 0.25 * product[32 * f : 32 * f + 32, LANES:]
+        ends.append(jnp.concatenate([end, end], axis=1))
+    quarters = []
+    for q in range(E // 2):
+        beyond = ends[1] if q == 0 else ends[0] if q == E // 2 - 1 else jnp.zeros_like(sides[0])
+        value = beyond
+        for f in range(4):
+            shift = (2 * E * f - 2 * E * q - (half if f >= 2 else 0)) % LANES
+            moved = pltpu.roll(sides[f], shift, 1) if shift else sides[f]
+            value = jnp.where((lane >= 2 * E * f) & (lane < 2 * E * (f + 1)), moved, value)
+        quarters.append(value)
+    return quarters
 
 
 def coarse_kernel(channels, arrived_ref, *refs):
-    out_refs, quarter_ref = refs[:4], refs[4]
+    out_refs, quarter_ref, axis_ref = refs[:4], refs[4], refs[5]
     tile_id = lax.axis_index("tile")
-    for which in range(2):
-        low, high, coords = unpack(arrived_ref, which, channels)
-        values = jnp.concatenate([low, high], axis=0)
-        own, skins = sample_weights(coords, which == 0)
-        product = contract_last(values, jnp.concatenate(own + skins, axis=0))
-        base = 16 * len(own)
-        for q, skin in enumerate(skin_quarters(product[:, base:])):
-            if which == 0:
-                quarter_ref[q, 0] = product[:, q * LANES : (q + 1) * LANES]
-            quarter_ref[q, 1 + which] = skin
+    half = LANES // 2
+    pairs = arrived_ref.shape[0] // 2
+
+    def blocks(which, make):
+        made = []
+        for p in range(pairs):
+            first = arrived_ref[p, which]
+            second = arrived_ref[p + pairs, which]
+            low = jnp.concatenate([first[:, :half], second[:, :half]], axis=1)
+            high = jnp.concatenate([first[:, half:], second[:, half:]], axis=1)
+            made.append(make(high.astype(jnp.float32)[8:], axis_ref.at[which, p], low, high))
+        return [[block[i] for block in made] for i in range(len(made[0]))]
+
+    left, right, folds = blocks(0, own_block)
+    product = contract_last(lay_out(left), lay_out(right))
+    ends = [block[:2] + block[-2:] for block in left]
+    folded = contract_last(lay_out(ends), lay_out(folds))
+    for q, (own, skin) in enumerate(own_quarters(product, folded)):
+        quarter_ref[q, 0] = own
+        quarter_ref[q, 1] = skin
+    left, right = blocks(1, skin_block)
+    for q, skin in enumerate(skin_quarters(contract_last(lay_out(left), lay_out(right)))):
+        quarter_ref[q, 2] = skin
     for delta in range(4):
         for part in range(3):
             out_refs[delta][part] = quarter_ref[tile_id ^ delta, part][:channels]
@@ -461,7 +535,7 @@
 def fine_kernel(channels, coarse_total, arrived_ref, near_ref, fine_ref, source_ref, turn_ref):
     first = lax.axis_index("brick") * CB_DEV - CB_DEV // 2
     lane = lax.broadcasted_iota(jnp.int32, (8, LANES), 1)
-    group = jnp.where(lane < LANES // 2, (lane // E) % 4, 4)
+    group = jnp.minimum(lane // (2 * E), 4)
     x_face = jnp.where(lax.axis_index("tile") < 2, 0, 1)
     for i in range(CB_DEV):
         near = [(near_ref[i, face] - first + coarse_total) % coarse_total for face in (3, 2, 5, 4, x_face)]
@@ -545,7 +619,7 @@
         sample_grad,
     )
     packed = pl.pallas_call(
-        functools.partial(pack_kernel, group_len, tuple(partners)),
+        functools.partial(pack_kernel, group_len, tile_count, tuple(partners)),
         out_shape=jax.ShapeDtypeStruct((dests, 2, 16, LANES), jnp.bfloat16),
         in_specs=[hbm] * 3,
         out_specs=vmem,
@@ -566,7 +640,10 @@
         out_shape=(message,) * 4,
         in_specs=[vmem],
         out_specs=(vmem,) * 4,
-        scratch_shapes=[pltpu.VMEM((4, 3, 32, LANES), jnp.float32)],
+        scratch_shapes=[
+            pltpu.VMEM((4, 3, 32, LANES), jnp.float32),
+            pltpu.VMEM((2, dests // 2, 3, 8, LANES), jnp.float32),
+        ],
         compiler_params=limit,
         name="coarse",
     )(arrived)

time: 30.9 us -> 30.1 us (0.974)
  Pallas kernels: 6.57 us -> 5.75 us
    pallas_call x1, Pallas kernels: 1.81 us -> 1.31 us  [family_body(): pl.pallas_call(functools.partial(coarse_kernel, channels), out_shape=(mes...]
    pallas_call x1, Pallas kernels: 1.68 us -> 1.36 us  [family_body(): pl.pallas_call(functools.partial(pack_kernel, group_len, tile_count, tupl...]
  transfers between devices with their start and end apart: 3 -> 3, of which waited for: 2 -> 2; matrix products, arithmetic and copies ran while one was open for 0% -> 0% of each run, Pallas kernels for 7% -> 8%
where the time goes in v4:
time: 30.1 us; the launch traced here: 29.8 us
  blocking collectives  17.4 us (58%)
  Pallas kernels  5.75 us (19%)
  starting transfers between devices  4.45 us (15%)
  waiting for transfers between devices  1.6 us (5%)
  between operations  0.66 us (2%)
    all_to_all x1, blocking collectives, family_body(): arrived = lax.all_to_all(packed, ('brick', 'tile'), 0, 0, tiled=True)  17.4 us
    ppermute x3, starting transfers between devices, family_body(): lax.ppermute(messages[delta], 'tile', [(t, t ^ delta) for t in range(tile...  4.45 us
    pallas_call x1, Pallas kernels, family_body(): pl.pallas_call(functools.partial(fine_kernel, channels, CB_DEV * owners),...  2.25 us
    ppermute x3, waiting for transfers between devices, family_body(): lax.ppermute(messages[delta], 'tile', [(t, t ^ delta) for t in range(tile...  1.6 us
    pallas_call x1, Pallas kernels, family_body(): pl.pallas_call(functools.partial(pack_kernel, group_len, tile_count, tupl...  1.36 us
    pallas_call x1, Pallas kernels, family_body(): pl.pallas_call(functools.partial(coarse_kernel, channels), out_shape=(mes...  1.31 us
    pallas_call x1, Pallas kernels, family_body(): pl.pallas_call(functools.partial(combine_kernel, channels), out_shape=jax...  0.82 us
  transfers between devices with their start and end apart: 3, of which 2 were waited for; matrix products, arithmetic and copies ran while one was open for 0% of the time, Pallas kernels for 8%

profile of v4, /device:TPU:0, one launch (start us, length us, event | category | flops | bytes accessed | tf_op | source)
XLA Modules:
  0.0 29.8 jit_solution(6659950188008415702)
XLA Ops:
  0.6 1.4 %pack.1 = bf16[32,2,16,128]{3,2,1,0:T(8,128)(2,1)S(1)} custom-call(s32[8,128]{1,0:T(8,128)} %bitcast.9, s32[8,128]{1,0:T(8,128)} %bitcast.10, bf16[28,1024]{1,0:T(8,128)(2,1)} %grad_hbm.1), custom_call_target="tpu_custom_call" | custom-call | tf_op jit(solution)/shard_map/pack/pallas_call | solution.py:621
  2.0 17.4 %all_to_all.5.arrived_ref = bf16[32,2,16,128]{3,2,1,0:T(8,128)(2,1)S(1)} all-to-all(bf16[32,2,16,128]{3,2,1,0:T(8,128)(2,1)S(1)} %pack.1), channel_id=1, replica_groups=mesh['brick'=8,'tile'=4] {'brick','tile'}, dimensions={0} | all-to-all | bytes 524288 | tf_op jit(solution)/shard_map/all_to_all | solution.py:636
  19.4 1.3 %coarse.1 = (f32[3,28,128]{2,1,0:T(8,128)S(1)}, f32[3,28,128]{2,1,0:T(8,128)S(1)}, f32[3,28,128]{2,1,0:T(8,128)S(1)}, f32[3,28,128]{2,1,0:T(8,128)S(1)}) custom-call(bf16[32,2,16,128]{3,2,1,0:T(8,128)(2,1)S(1)} %all_to_all.5.arrived_ref), custom_call_target="tpu_custom_call" | custom-call | tf_op jit(solution)/shard_map/coarse/pallas_call | solution.py:638
  20.7 0.0 copy-start.1
  20.7 0.8 %collective-permute-start = (f32[3,28,128]{2,1,0:T(8,128)S(1)}, f32[3,28,128]{2,1,0:T(8,128)S(1)}, u32[]{:S(2)}, u32[]{:S(2)}) collective-permute-start(f32[3,28,128]{2,1,0:T(8,128)S(1)} %get-tuple-element.11), channel_id=1, source_target_pairs={{0,1},{1,0},{2,3},{3,2},{4,5},{5,4},{6,7},{7,6},{8,9},{9,8},{10,11... | collective-permute-start | bytes 129032 | tf_op jit(solution)/shard_map/ppermute | solution.py:652
  21.5 1.6 %collective-permute-start.1 = (f32[3,28,128]{2,1,0:T(8,128)S(1)}, f32[3,28,128]{2,1,0:T(8,128)S(1)}, u32[]{:S(2)}, u32[]{:S(2)}) collective-permute-start(f32[3,28,128]{2,1,0:T(8,128)S(1)} %get-tuple-element.12), channel_id=1, source_target_pairs={{0,2},{1,3},{2,0},{3,1},{4,6},{5,7},{6,4},{7,5},{8,10},{9,11},{10,... | collective-permute-start | bytes 129032 | tf_op jit(solution)/shard_map/ppermute | solution.py:652
  23.0 0.0 copy-start
  23.0 2.1 %collective-permute-start.2 = (f32[3,28,128]{2,1,0:T(8,128)S(1)}, f32[3,28,128]{2,1,0:T(8,128)S(1)}, u32[]{:S(2)}, u32[]{:S(2)}) collective-permute-start(f32[3,28,128]{2,1,0:T(8,128)S(1)} %get-tuple-element.13), channel_id=1, source_target_pairs={{0,3},{1,2},{2,1},{3,0},{4,7},{5,6},{6,5},{7,4},{8,11},{9,10},{10,... | collective-permute-start | bytes 129032 | tf_op jit(solution)/shard_map/ppermute | solution.py:652
  25.1 0.0 copy-done.1
  25.2 2.3 %fine.1 = (f32[224,512]{1,0:T(8,128)}, s32[4,8,128]{2,1,0:T(8,128)S(1)}) custom-call(bf16[32,2,16,128]{3,2,1,0:T(8,128)(2,1)S(1)} %all_to_all.5.arrived_ref, s32[4,6]{1,0:T(4,128)S(1)} %copy-done.1), custom_call_target="tpu_custom_call" | custom-call | tf_op jit(solution)/shard_map/fine/pallas_call | solution.py:653
  27.4 0.0 collective-permute-done.one_ref
  27.4 0.6 %collective-permute-done.1.two_ref = f32[3,28,128]{2,1,0:T(8,128)S(1)} collective-permute-done((f32[3,28,128]{2,1,0:T(8,128)S(1)}, f32[3,28,128]{2,1,0:T(8,128)S(1)}, u32[]{:S(2)}, u32[]{:S(2)}) %collective-permute-start.1) | collective-permute-done | bytes 43040 | tf_op jit(solution)/shard_map/ppermute | solution.py:652
  28.0 1.0 %collective-permute-done.2.three_ref = f32[3,28,128]{2,1,0:T(8,128)S(1)} collective-permute-done((f32[3,28,128]{2,1,0:T(8,128)S(1)}, f32[3,28,128]{2,1,0:T(8,128)S(1)}, u32[]{:S(2)}, u32[]{:S(2)}) %collective-permute-start.2) | collective-permute-done | bytes 43040 | tf_op jit(solution)/shard_map/ppermute | solution.py:652
  29.0 0.0 copy-done
  29.0 0.8 %combine.1 = f32[112,128]{1,0:T(8,128)} custom-call(s32[4,8,128]{2,1,0:T(8,128)S(1)} %get-tuple-element.9.source_ref, f32[3,28,128]{2,1,0:T(8,128)S(1)} %get-tuple-element.10.zero_ref, f32[3,28,128]{2,1,0:T(8,128)S(1)} %collective-permute-done.one_ref, f32[3,28,128]{2,1,0:T(8,128)S(1)} %collective-permute-done.1.two_ref, ...), custom_call_target="tpu_custom_call" | custom-call | tf_op jit(solution)/shard_map/combine/pallas_call | solution.py:665
Async XLA Ops:
  20.7 4.5 %copy-start.1 = (s32[4,6]{1,0:T(4,128)S(1)}, s32[4,6]{1,0:T(4,128)}, u32[]{:S(2)}) copy-start(s32[4,6]{1,0:T(4,128)} %near_ref.1) | copy-start | bytes 292
  20.7 6.7 %collective-permute-start = (f32[3,28,128]{2,1,0:T(8,128)S(1)}, f32[3,28,128]{2,1,0:T(8,128)S(1)}, u32[]{:S(2)}, u32[]{:S(2)}) collective-permute-start(f32[3,28,128]{2,1,0:T(8,128)S(1)} %get-tuple-element.11), channel_id=1, source_target_pairs={{0,1},{1,0},{2,3},{3,2},{4,5},{5,4},{6,7},{7,6},{8,9},{9,8},{10,11... | collective-permute-start | bytes 129032 | tf_op jit(solution)/shard_map/ppermute | solution.py:652
  21.5 6.6 %collective-permute-start.1 = (f32[3,28,128]{2,1,0:T(8,128)S(1)}, f32[3,28,128]{2,1,0:T(8,128)S(1)}, u32[]{:S(2)}, u32[]{:S(2)}) collective-permute-start(f32[3,28,128]{2,1,0:T(8,128)S(1)} %get-tuple-element.12), channel_id=1, source_target_pairs={{0,2},{1,3},{2,0},{3,1},{4,6},{5,7},{6,4},{7,5},{8,10},{9,11},{10,... | collective-permute-start | bytes 129032 | tf_op jit(solution)/shard_map/ppermute | solution.py:652
  23.0 6.0 %copy-start = (bf16[2,128,128]{2,1,0:T(8,128)(2,1)S(1)}, bf16[2,128,128]{2,1,0:T(8,128)(2,1)}, u32[]{:S(2)}) copy-start(bf16[2,128,128]{2,1,0:T(8,128)(2,1)} %constant.2.clone.table_ref) | copy-start | bytes 196612
  23.0 6.0 %collective-permute-start.2 = (f32[3,28,128]{2,1,0:T(8,128)S(1)}, f32[3,28,128]{2,1,0:T(8,128)S(1)}, u32[]{:S(2)}, u32[]{:S(2)}) collective-permute-start(f32[3,28,128]{2,1,0:T(8,128)S(1)} %get-tuple-element.13), channel_id=1, source_target_pairs={{0,3},{1,2},{2,1},{3,0},{4,7},{5,6},{6,5},{7,4},{8,11},{9,10},{10,... | collective-permute-start | bytes 129032 | tf_op jit(solution)/shard_map/ppermute | solution.py:652

commit v5 on v4

--- a/solution.py
+++ b/solution.py
@@ -253,13 +253,31 @@
     for side in range(2):
         for odd in range(2):
             for at in range(brick_edge):
-                base = odd * brick_edge + at
+                base = odd * 4 * brick_edge + at
                 out[side, base, odd * square + last * brick_edge + at] = 1
-                out[side, base + 2 * brick_edge, odd * square + at] = 1
-                out[side, base + 4 * brick_edge, odd * square + at * brick_edge + last] = 1
-                out[side, base + 6 * brick_edge, odd * square + at * brick_edge] = 1
+                out[side, base + brick_edge, odd * square + at] = 1
+                out[side, base + 2 * brick_edge, odd * square + at * brick_edge + last] = 1
+                out[side, base + 3 * brick_edge, odd * square + at * brick_edge] = 1
         for cell in range(square):
             out[side, square + cell, side * square + cell] = 1
+    return out
+
+
+def fold_table(brick_edge):
+    square = brick_edge * brick_edge
+    last = brick_edge - 1
+    base = square
+    out = np.zeros((LANES, 2 * LANES), np.float32)
+    for at in range(brick_edge):
+        targets = [(at, at), (brick_edge + at, last * brick_edge + at)]
+        if 0 < at < last:
+            targets += [(2 * brick_edge + at, at * brick_edge), (3 * brick_edge + at, at * brick_edge + last)]
+        else:
+            out[base + 2 * brick_edge + at, LANES + square + at * brick_edge] = -1
+            out[base + 3 * brick_edge + at, LANES + square + at * brick_edge + last] = -1
+        for source, cell in targets:
+            out[base + source, cell] = 1
+            out[base + source, square + cell] = 1
     return out
 
 
@@ -397,10 +415,9 @@
     return row, coords, rows
 
 
-def paired(axis_ref, at, rows):
+def lines_of(axis_ref, at, rows):
     axis_ref[at] = rows
-    lines = [axis_ref[at, pl.ds(m, 8, stride=0), :] for m in range(E)]
-    return [pack_pair(lines[2 * g], lines[2 * g + 1]) for g in range(E // 2)]
+    return [axis_ref[at, pl.ds(m, 8, stride=0), :] for m in range(E)]
 
 
 def select_rows(hits, low, high):
@@ -415,32 +432,46 @@
     row, (x, y, z), (_, y_rows, z_rows) = block_axes(code, axis_ref)
     last = 2.0 * E - 1.0
     blank = jnp.zeros((8, LANES), jnp.float32)
-    y_pair = paired(axis_ref, 2, y_rows)
+    y_lines = lines_of(axis_ref, 2, y_rows)
+    y_pair = [pack_pair(y_lines[2 * g], y_lines[2 * g + 1]) for g in range(E // 2)]
     z_in = pack_pair(z_rows, z_rows)
     y_low = jnp.where(y == 0.0, 0.25, 0.0)
     y_high = jnp.where(y == last, 0.25, 0.0)
     z_low = jnp.where(z == 0.0, 0.25, 0.0)
     z_high = jnp.where(z == last, 0.25, 0.0)
     z_out = jnp.where(row == 0.0, z_low, jnp.where(row == E - 1.0, z_high, blank))
-    z_out = pack_pair(z_out, z_out)
-    z_both = z_in + z_out
-    plane = [y_pair[g] * z_in for g in range(E // 2)]
-    inner = list(plane)
-    outer = [y_pair[g] * z_out for g in range(E // 2)]
-    for g, y_out in ((0, pack_pair(y_low, blank)), (E // 2 - 1, pack_pair(blank, y_high))):
-        inner[g] = inner[g] + y_out * z_out
-        outer[g] = outer[g] + y_out * z_both
-    faces = [y_low * z_rows, y_high * z_rows, z_low * y_rows, z_high * y_rows]
-    x16 = pack_pair(x, x)
-    left = select_rows([x16 == jnp.bfloat16(at) for at in range(2 * E)], low, high)
-    return left, inner + [pack_pair(face, blank) for face in faces], outer + plane
+    y_edge = jnp.where(row == 0.0, y_low, jnp.where(row == E - 1.0, y_high, y_rows))
+    z_both = z_rows + z_out
+    inner = [value * z_in for value in y_pair]
+    inner[0] = inner[0] + pack_pair(y_low * z_out, blank)
+    inner[-1] = inner[-1] + pack_pair(blank, y_high * z_out)
+    faces = [pack_pair(y_low * z_rows, y_high * z_rows), pack_pair(z_low * y_rows, z_high * y_rows)]
+    edges = [
+        pack_pair(y_lines[0] * z_out + y_low * z_both, y_lines[E - 1] * z_out + y_high * z_both),
+        pack_pair(y_edge * z_low, y_edge * z_high),
+    ]
+    whole = x.astype(jnp.int32)
+    pair_of = (whole >> 1).astype(jnp.float32)
+    odd = (whole & 1).astype(jnp.float32)
+    odd16 = pack_pair(odd, odd)
+    even16 = jnp.bfloat16(1.0) - odd16
+    ends = jnp.where((x == 0.0) | (x == last), 1.0, 0.0)
+    ends16 = pack_pair(ends, ends)
+    pair16 = pack_pair(pair_of, pair_of)
+    left = select_rows([pair16 == jnp.bfloat16(at) for at in range(E)], low, high)
+    right = [value * even16 for value in inner] + [value * odd16 for value in inner]
+    right += [value * even16 for value in faces] + [value * odd16 for value in faces]
+    return left, right + [value * ends16 for value in edges]
 
 
 def skin_block(code, axis_ref, low, high):
     _, coords, (x_rows, y_rows, z_rows) = block_axes(code, axis_ref)
     last = 2 * E - 1
-    x_pair = paired(axis_ref, 1, x_rows)
-    y_pair = paired(axis_ref, 2, y_rows)
+    x_lines = lines_of(axis_ref, 1, x_rows)
+    y_lines = lines_of(axis_ref, 2, y_rows)
+    x_order = list(range(0, E, 2)) + list(range(1, E, 2))
+    x_pair = [pack_pair(x_lines[x_order[2 * g]], x_lines[x_order[2 * g + 1]]) for g in range(E // 2)]
+    y_pair = [pack_pair(y_lines[2 * g], y_lines[2 * g + 1]) for g in range(E // 2)]
     z_in = pack_pair(z_rows, z_rows)
     y_in = pack_pair(y_rows, y_rows)
     x16, y16, z16 = [pack_pair(c, c) for c in coords]
@@ -456,34 +487,46 @@
     )
 
 
-def own_quarters(product, folds):
+def own_quarters(product, table):
     half = LANES // 2
+    width = half // 2
     lane = lax.broadcasted_iota(jnp.int32, (32, LANES), 1)
     left = lane < half
-    at_x = [product[32 * at : 32 * at + 32] for at in range(2 * E)]
-    first, second = 0.25 * folds[:32], 0.25 * folds[32:]
-    layers = []
-    for m in range(E):
-        value = 0.75 * (at_x[2 * m] + at_x[2 * m + 1])
-        if m == 0:
-            value = value + 0.25 * at_x[2] + jnp.where(left, first, 0.0)
-        elif m == E - 1:
-            value = value + 0.25 * at_x[2 * m - 1] + jnp.where(left, second, 0.0)
-        else:
-            value = value + 0.25 * (at_x[2 * m - 1] + at_x[2 * m + 2])
-        layers.append(value)
+    blank = jnp.zeros((32, LANES - product.shape[1] % LANES), jnp.float32)
+    cells = [product[32 * i : 32 * i + 32, :LANES] for i in range(E)]
+    faces = [jnp.concatenate([product[32 * i : 32 * i + 32, LANES:], blank], axis=1) for i in range(E)]
+    high_part, low_part = split_two(jnp.concatenate([faces[0], faces[-1]], axis=0))
+    folds = jnp.dot(high_part, table, preferred_element_type=jnp.float32)
+    folds = 0.25 * (folds + jnp.dot(low_part, table, preferred_element_type=jnp.float32))
+    cells_turned = [pltpu.roll(value, half, 1) for value in cells]
+    faces_turned = [pltpu.roll(value, LANES - width, 1) for value in faces]
+
+    def mixed(m, even, odd):
+        near = [odd[m - 1]] if m > 0 else []
+        near += [even[m + 1]] if m < E - 1 else []
+        return 0.75 * (even[m] + odd[m]) + 0.25 * (near[0] if len(near) == 1 else near[0] + near[1])
+
     quarters = []
     for q in range(E // 2):
-        even, odd = layers[2 * q], layers[2 * q + 1]
-        faces = pltpu.roll(even, half, 1) + pltpu.roll(jnp.where(left, 0.0, odd), half + E, 1)
-        beyond = second if q == 0 else first if q == E // 2 - 1 else jnp.zeros_like(even)
-        quarters.append((jnp.where(left, even, pltpu.roll(odd, half, 1)), jnp.where(left, faces, beyond)))
+        first = mixed(2 * q, cells, cells_turned)
+        second = mixed(2 * q + 1, cells_turned, cells)
+        beyond = jnp.zeros_like(first)
+        if q == 0:
+            first = first + folds[:32, :LANES]
+            beyond = 0.25 * cells[-1] + folds[32:, LANES:]
+        if q == E // 2 - 1:
+            second = second + folds[32:, :LANES]
+            beyond = 0.25 * cells_turned[0] + folds[:32, LANES:]
+        side = pltpu.roll(mixed(2 * q + 1, faces, faces_turned), width, 1)
+        skin = jnp.where(lane < width, mixed(2 * q, faces, faces_turned), jnp.where(left, side, beyond))
+        quarters.append((jnp.where(left, first, second), skin))
     return quarters
 
 
 def skin_quarters(product):
     half = LANES // 2
     lane = lax.broadcasted_iota(jnp.int32, (32, LANES), 1)
+    face_of = jnp.where(lane < half, (lane // E) % 4, 4)
     sides = [0.25 * product[32 * f : 32 * f + 32, :LANES] for f in range(4)]
     ends = []
     for f in (4, 5):
@@ -491,18 +534,19 @@
         ends.append(jnp.concatenate([end, end], axis=1))
     quarters = []
     for q in range(E // 2):
-        beyond = ends[1] if q == 0 else ends[0] if q == E // 2 - 1 else jnp.zeros_like(sides[0])
-        value = beyond
+        value = ends[1] if q == 0 else ends[0] if q == E // 2 - 1 else jnp.zeros_like(sides[0])
         for f in range(4):
-            shift = (2 * E * f - 2 * E * q - (half if f >= 2 else 0)) % LANES
+            shift = (E * (f - q) - (half if f >= 2 else 0)) % LANES
             moved = pltpu.roll(sides[f], shift, 1) if shift else sides[f]
-            value = jnp.where((lane >= 2 * E * f) & (lane < 2 * E * (f + 1)), moved, value)
+            value = jnp.where(face_of == f, moved, value)
         quarters.append(value)
     return quarters
 
 
-def coarse_kernel(channels, arrived_ref, *refs):
-    out_refs, quarter_ref, axis_ref = refs[:4], refs[4], refs[5]
+def coarse_kernel(channels, arrived_ref, table_hbm, *refs):
+    out_refs, (quarter_ref, axis_ref, table_ref, sem) = refs[:4], refs[4:]
+    table_copy = pltpu.make_async_copy(table_hbm, table_ref, sem)
+    table_copy.start()
     tile_id = lax.axis_index("tile")
     half = LANES // 2
     pairs = arrived_ref.shape[0] // 2
@@ -517,16 +561,20 @@
             made.append(make(high.astype(jnp.float32)[8:], axis_ref.at[which, p], low, high))
         return [[block[i] for block in made] for i in range(len(made[0]))]
 
-    left, right, folds = blocks(0, own_block)
-    product = contract_last(lay_out(left), lay_out(right))
-    ends = [block[:2] + block[-2:] for block in left]
-    folded = contract_last(lay_out(ends), lay_out(folds))
-    for q, (own, skin) in enumerate(own_quarters(product, folded)):
+    def in_halves(left, right):
+        middle = pairs // 2
+        return contract_last(lay_out(left[:middle]), lay_out(right[:middle])) + contract_last(
+            lay_out(left[middle:]), lay_out(right[middle:])
+        )
+
+    skin_product = in_halves(*blocks(1, skin_block))
+    own_product = in_halves(*blocks(0, own_block))
+    for q, skin in enumerate(skin_quarters(skin_product)):
+        quarter_ref[q, 2] = skin
+    table_copy.wait()
+    for q, (own, skin) in enumerate(own_quarters(own_product, table_ref[...])):
         quarter_ref[q, 0] = own
         quarter_ref[q, 1] = skin
-    left, right = blocks(1, skin_block)
-    for q, skin in enumerate(skin_quarters(contract_last(lay_out(left), lay_out(right)))):
-        quarter_ref[q, 2] = skin
     for delta in range(4):
         for part in range(3):
             out_refs[delta][part] = quarter_ref[tile_id ^ delta, part][:channels]
@@ -535,7 +583,7 @@
 def fine_kernel(channels, coarse_total, arrived_ref, near_ref, fine_ref, source_ref, turn_ref):
     first = lax.axis_index("brick") * CB_DEV - CB_DEV // 2
     lane = lax.broadcasted_iota(jnp.int32, (8, LANES), 1)
-    group = jnp.minimum(lane // (2 * E), 4)
+    group = jnp.where(lane < LANES // 2, (lane // E) % 4, 4)
     x_face = jnp.where(lax.axis_index("tile") < 2, 0, 1)
     for i in range(CB_DEV):
         near = [(near_ref[i, face] - first + coarse_total) % coarse_total for face in (3, 2, 5, 4, x_face)]
@@ -638,15 +686,17 @@
     messages = pl.pallas_call(
         functools.partial(coarse_kernel, channels),
         out_shape=(message,) * 4,
-        in_specs=[vmem],
+        in_specs=[vmem, hbm],
         out_specs=(vmem,) * 4,
         scratch_shapes=[
             pltpu.VMEM((4, 3, 32, LANES), jnp.float32),
             pltpu.VMEM((2, dests // 2, 3, 8, LANES), jnp.float32),
+            pltpu.VMEM((LANES, 2 * LANES), jnp.bfloat16),
+            pltpu.SemaphoreType.DMA,
         ],
         compiler_params=limit,
         name="coarse",
-    )(arrived)
+    )(arrived, pltpu.with_memory_space_constraint(jnp.asarray(fold_table(E), jnp.bfloat16), pltpu.HBM))
     arrivals = {}
     for delta in (3, 1, 2):
         arrivals[delta] = lax.ppermute(messages[delta], "tile", [(t, t ^ delta) for t in range(tile_count)])

time: 30.1 us -> 29.8 us (0.990)
  no operation moved by 1% of the time
where the time goes in v5:
time: 29.8 us; the launch traced here: 29.6 us
  blocking collectives  17.4 us (58%)
  Pallas kernels  5.49 us (18%)
  starting transfers between devices  4.45 us (15%)
  waiting for transfers between devices  1.6 us (5%)
  between operations  0.66 us (2%)
    all_to_all x1, blocking collectives, family_body(): arrived = lax.all_to_all(packed, ('brick', 'tile'), 0, 0, tiled=True)  17.4 us
    ppermute x3, starting transfers between devices, family_body(): lax.ppermute(messages[delta], 'tile', [(t, t ^ delta) for t in range(tile...  4.45 us
    pallas_call x1, Pallas kernels, family_body(): pl.pallas_call(functools.partial(fine_kernel, channels, CB_DEV * owners),...  2.25 us
    ppermute x3, waiting for transfers between devices, family_body(): lax.ppermute(messages[delta], 'tile', [(t, t ^ delta) for t in range(tile...  1.6 us
    pallas_call x1, Pallas kernels, family_body(): pl.pallas_call(functools.partial(pack_kernel, group_len, tile_count, tupl...  1.36 us
    pallas_call x1, Pallas kernels, family_body(): pl.pallas_call(functools.partial(coarse_kernel, channels), out_shape=(mes...  1.05 us
    pallas_call x1, Pallas kernels, family_body(): pl.pallas_call(functools.partial(combine_kernel, channels), out_shape=jax...  0.82 us
  transfers between devices with their start and end apart: 3, of which 2 were waited for; matrix products, arithmetic and copies ran while one was open for 0% of the time, Pallas kernels for 8%

profile of v5, /device:TPU:0, one launch (start us, length us, event | category | flops | bytes accessed | tf_op | source)
XLA Modules:
  0.0 29.6 jit_solution(16611318858369275184)
XLA Ops:
  0.6 1.4 %pack.1 = bf16[32,2,16,128]{3,2,1,0:T(8,128)(2,1)S(1)} custom-call(s32[8,128]{1,0:T(8,128)} %bitcast.9, s32[8,128]{1,0:T(8,128)} %bitcast.10, bf16[28,1024]{1,0:T(8,128)(2,1)} %grad_hbm.1), custom_call_target="tpu_custom_call" | custom-call | tf_op jit(solution)/shard_map/pack/pallas_call | solution.py:669
  2.0 17.4 %all_to_all.5.arrived_ref = bf16[32,2,16,128]{3,2,1,0:T(8,128)(2,1)S(1)} all-to-all(bf16[32,2,16,128]{3,2,1,0:T(8,128)(2,1)S(1)} %pack.1), channel_id=1, replica_groups=mesh['brick'=8,'tile'=4] {'brick','tile'}, dimensions={0} | all-to-all | bytes 524288 | tf_op jit(solution)/shard_map/all_to_all | solution.py:684
  19.4 1.1 %coarse.1 = (f32[3,28,128]{2,1,0:T(8,128)S(1)}, f32[3,28,128]{2,1,0:T(8,128)S(1)}, f32[3,28,128]{2,1,0:T(8,128)S(1)}, f32[3,28,128]{2,1,0:T(8,128)S(1)}) custom-call(bf16[32,2,16,128]{3,2,1,0:T(8,128)(2,1)S(1)} %all_to_all.5.arrived_ref, bf16[128,256]{1,0:T(8,128)(2,1)} %constant.4.clone.table_hbm), custom_call_target="tpu_custom_call" | custom-call | tf_op jit(solution)/shard_map/coarse/pallas_call | solution.py:686
  20.4 0.0 copy-start.1
  20.4 0.8 %collective-permute-start = (f32[3,28,128]{2,1,0:T(8,128)S(1)}, f32[3,28,128]{2,1,0:T(8,128)S(1)}, u32[]{:S(2)}, u32[]{:S(2)}) collective-permute-start(f32[3,28,128]{2,1,0:T(8,128)S(1)} %get-tuple-element.11), channel_id=1, source_target_pairs={{0,1},{1,0},{2,3},{3,2},{4,5},{5,4},{6,7},{7,6},{8,9},{9,8},{10,11... | collective-permute-start | bytes 129032 | tf_op jit(solution)/shard_map/ppermute | solution.py:702
  21.2 1.6 %collective-permute-start.1 = (f32[3,28,128]{2,1,0:T(8,128)S(1)}, f32[3,28,128]{2,1,0:T(8,128)S(1)}, u32[]{:S(2)}, u32[]{:S(2)}) collective-permute-start(f32[3,28,128]{2,1,0:T(8,128)S(1)} %get-tuple-element.12), channel_id=1, source_target_pairs={{0,2},{1,3},{2,0},{3,1},{4,6},{5,7},{6,4},{7,5},{8,10},{9,11},{10,... | collective-permute-start | bytes 129032 | tf_op jit(solution)/shard_map/ppermute | solution.py:702
  22.8 0.0 copy-start
  22.8 2.1 %collective-permute-start.2 = (f32[3,28,128]{2,1,0:T(8,128)S(1)}, f32[3,28,128]{2,1,0:T(8,128)S(1)}, u32[]{:S(2)}, u32[]{:S(2)}) collective-permute-start(f32[3,28,128]{2,1,0:T(8,128)S(1)} %get-tuple-element.13), channel_id=1, source_target_pairs={{0,3},{1,2},{2,1},{3,0},{4,7},{5,6},{6,5},{7,4},{8,11},{9,10},{10,... | collective-permute-start | bytes 129032 | tf_op jit(solution)/shard_map/ppermute | solution.py:702
  24.9 0.0 copy-done.1
  24.9 2.3 %fine.1 = (f32[224,512]{1,0:T(8,128)}, s32[4,8,128]{2,1,0:T(8,128)S(1)}) custom-call(bf16[32,2,16,128]{3,2,1,0:T(8,128)(2,1)S(1)} %all_to_all.5.arrived_ref, s32[4,6]{1,0:T(4,128)S(1)} %copy-done.1), custom_call_target="tpu_custom_call" | custom-call | tf_op jit(solution)/shard_map/fine/pallas_call | solution.py:703
  27.1 0.0 collective-permute-done.one_ref
  27.1 0.6 %collective-permute-done.1.two_ref = f32[3,28,128]{2,1,0:T(8,128)S(1)} collective-permute-done((f32[3,28,128]{2,1,0:T(8,128)S(1)}, f32[3,28,128]{2,1,0:T(8,128)S(1)}, u32[]{:S(2)}, u32[]{:S(2)}) %collective-permute-start.1) | collective-permute-done | bytes 43040 | tf_op jit(solution)/shard_map/ppermute | solution.py:702
  27.8 1.0 %collective-permute-done.2.three_ref = f32[3,28,128]{2,1,0:T(8,128)S(1)} collective-permute-done((f32[3,28,128]{2,1,0:T(8,128)S(1)}, f32[3,28,128]{2,1,0:T(8,128)S(1)}, u32[]{:S(2)}, u32[]{:S(2)}) %collective-permute-start.2) | collective-permute-done | bytes 43040 | tf_op jit(solution)/shard_map/ppermute | solution.py:702
  28.7 0.0 copy-done
  28.8 0.8 %combine.1 = f32[112,128]{1,0:T(8,128)} custom-call(s32[4,8,128]{2,1,0:T(8,128)S(1)} %get-tuple-element.9.source_ref, f32[3,28,128]{2,1,0:T(8,128)S(1)} %get-tuple-element.10.zero_ref, f32[3,28,128]{2,1,0:T(8,128)S(1)} %collective-permute-done.one_ref, f32[3,28,128]{2,1,0:T(8,128)S(1)} %collective-permute-done.1.two_ref, ...), custom_call_target="tpu_custom_call" | custom-call | tf_op jit(solution)/shard_map/combine/pallas_call | solution.py:715
Async XLA Ops:
  20.4 4.5 %copy-start.1 = (s32[4,6]{1,0:T(4,128)S(1)}, s32[4,6]{1,0:T(4,128)}, u32[]{:S(2)}) copy-start(s32[4,6]{1,0:T(4,128)} %near_ref.1) | copy-start | bytes 292
  20.4 6.7 %collective-permute-start = (f32[3,28,128]{2,1,0:T(8,128)S(1)}, f32[3,28,128]{2,1,0:T(8,128)S(1)}, u32[]{:S(2)}, u32[]{:S(2)}) collective-permute-start(f32[3,28,128]{2,1,0:T(8,128)S(1)} %get-tuple-element.11), channel_id=1, source_target_pairs={{0,1},{1,0},{2,3},{3,2},{4,5},{5,4},{6,7},{7,6},{8,9},{9,8},{10,11... | collective-permute-start | bytes 129032 | tf_op jit(solution)/shard_map/ppermute | solution.py:702
  21.2 6.6 %collective-permute-start.1 = (f32[3,28,128]{2,1,0:T(8,128)S(1)}, f32[3,28,128]{2,1,0:T(8,128)S(1)}, u32[]{:S(2)}, u32[]{:S(2)}) collective-permute-start(f32[3,28,128]{2,1,0:T(8,128)S(1)} %get-tuple-element.12), channel_id=1, source_target_pairs={{0,2},{1,3},{2,0},{3,1},{4,6},{5,7},{6,4},{7,5},{8,10},{9,11},{10,... | collective-permute-start | bytes 129032 | tf_op jit(solution)/shard_map/ppermute | solution.py:702
  22.8 6.0 %copy-start = (bf16[2,128,128]{2,1,0:T(8,128)(2,1)S(1)}, bf16[2,128,128]{2,1,0:T(8,128)(2,1)}, u32[]{:S(2)}) copy-start(bf16[2,128,128]{2,1,0:T(8,128)(2,1)} %constant.5.clone.table_ref) | copy-start | bytes 196612
  22.8 6.0 %collective-permute-start.2 = (f32[3,28,128]{2,1,0:T(8,128)S(1)}, f32[3,28,128]{2,1,0:T(8,128)S(1)}, u32[]{:S(2)}, u32[]{:S(2)}) collective-permute-start(f32[3,28,128]{2,1,0:T(8,128)S(1)} %get-tuple-element.13), channel_id=1, source_target_pairs={{0,3},{1,2},{2,1},{3,0},{4,7},{5,6},{6,5},{7,4},{8,11},{9,10},{10,... | collective-permute-start | bytes 129032 | tf_op jit(solution)/shard_map/ppermute | solution.py:702

commit v6 on v5

--- a/solution.py
+++ b/solution.py
@@ -246,6 +246,10 @@
 KERNEL_VMEM = 16 * 1024 * 1024
 
 
+def beyond_lane(cell):
+    return cell + (32 if cell < 32 else 64)
+
+
 def expand_tables(brick_edge):
     square = brick_edge * brick_edge
     last = brick_edge - 1
@@ -253,28 +257,28 @@
     for side in range(2):
         for odd in range(2):
             for at in range(brick_edge):
-                base = odd * 4 * brick_edge + at
+                base = odd * square + at
                 out[side, base, odd * square + last * brick_edge + at] = 1
                 out[side, base + brick_edge, odd * square + at] = 1
                 out[side, base + 2 * brick_edge, odd * square + at * brick_edge + last] = 1
                 out[side, base + 3 * brick_edge, odd * square + at * brick_edge] = 1
         for cell in range(square):
-            out[side, square + cell, side * square + cell] = 1
+            out[side, beyond_lane(cell), side * square + cell] = 1
     return out
 
 
 def fold_table(brick_edge):
     square = brick_edge * brick_edge
     last = brick_edge - 1
-    base = square
+    base = 4 * brick_edge
     out = np.zeros((LANES, 2 * LANES), np.float32)
     for at in range(brick_edge):
         targets = [(at, at), (brick_edge + at, last * brick_edge + at)]
         if 0 < at < last:
             targets += [(2 * brick_edge + at, at * brick_edge), (3 * brick_edge + at, at * brick_edge + last)]
         else:
-            out[base + 2 * brick_edge + at, LANES + square + at * brick_edge] = -1
-            out[base + 3 * brick_edge + at, LANES + square + at * brick_edge + last] = -1
+            out[base + 2 * brick_edge + at, LANES + beyond_lane(at * brick_edge)] = -1
+            out[base + 3 * brick_edge + at, LANES + beyond_lane(at * brick_edge + last)] = -1
         for source, cell in targets:
             out[base + source, cell] = 1
             out[base + source, square + cell] = 1
@@ -460,8 +464,8 @@
     pair16 = pack_pair(pair_of, pair_of)
     left = select_rows([pair16 == jnp.bfloat16(at) for at in range(E)], low, high)
     right = [value * even16 for value in inner] + [value * odd16 for value in inner]
-    right += [value * even16 for value in faces] + [value * odd16 for value in faces]
-    return left, right + [value * ends16 for value in edges]
+    right += [value * even16 for value in faces] + [value * ends16 for value in edges]
+    return left, right + [value * odd16 for value in faces]
 
 
 def skin_block(code, axis_ref, low, high):
@@ -477,7 +481,9 @@
     x16, y16, z16 = [pack_pair(c, c) for c in coords]
     hits = [c == jnp.bfloat16(end) for c in (y16, z16, x16) for end in (0, last)]
     left = select_rows(hits, low, high)
-    right = [value * z_in for value in x_pair] + [value * y_in for value in x_pair]
+    right = []
+    for part in (x_pair[: E // 4], x_pair[E // 4 :]):
+        right += [value * z_in for value in part] + [value * y_in for value in part]
     return left, right + [value * z_in for value in y_pair]
 
 
@@ -489,54 +495,60 @@
 
 def own_quarters(product, table):
     half = LANES // 2
-    width = half // 2
     lane = lax.broadcasted_iota(jnp.int32, (32, LANES), 1)
     left = lane < half
+    spare = lane % half >= half // 2
     blank = jnp.zeros((32, LANES - product.shape[1] % LANES), jnp.float32)
     cells = [product[32 * i : 32 * i + 32, :LANES] for i in range(E)]
     faces = [jnp.concatenate([product[32 * i : 32 * i + 32, LANES:], blank], axis=1) for i in range(E)]
     high_part, low_part = split_two(jnp.concatenate([faces[0], faces[-1]], axis=0))
     folds = jnp.dot(high_part, table, preferred_element_type=jnp.float32)
     folds = 0.25 * (folds + jnp.dot(low_part, table, preferred_element_type=jnp.float32))
-    cells_turned = [pltpu.roll(value, half, 1) for value in cells]
-    faces_turned = [pltpu.roll(value, LANES - width, 1) for value in faces]
-
-    def mixed(m, even, odd):
-        near = [odd[m - 1]] if m > 0 else []
-        near += [even[m + 1]] if m < E - 1 else []
-        return 0.75 * (even[m] + odd[m]) + 0.25 * (near[0] if len(near) == 1 else near[0] + near[1])
+
+    def even_x(values, m):
+        return 0.75 * values[m] + 0.25 * values[m + 1] if m < E - 1 else 0.75 * values[m]
+
+    def odd_x(values, m):
+        return 0.75 * values[m] + 0.25 * values[m - 1] if m > 0 else 0.75 * values[m]
+
+    def layers(values, m):
+        stay = jnp.where(left, even_x(values, m), odd_x(values, m + 1))
+        cross = jnp.where(left, even_x(values, m + 1), odd_x(values, m))
+        return stay + pltpu.roll(cross, half, 1)
 
     quarters = []
     for q in range(E // 2):
-        first = mixed(2 * q, cells, cells_turned)
-        second = mixed(2 * q + 1, cells_turned, cells)
-        beyond = jnp.zeros_like(first)
+        own = layers(cells, 2 * q)
+        skin = layers(faces, 2 * q)
+        beyond = jnp.zeros_like(own)
         if q == 0:
-            first = first + folds[:32, :LANES]
-            beyond = 0.25 * cells[-1] + folds[32:, LANES:]
+            own = own + jnp.where(left, folds[:32, :LANES], 0.0)
+            moved = jnp.where(left, pltpu.roll(cells[-1], LANES - half // 2, 1), cells[-1])
+            beyond = 0.25 * moved + folds[32:, LANES:]
         if q == E // 2 - 1:
-            second = second + folds[32:, :LANES]
-            beyond = 0.25 * cells_turned[0] + folds[:32, LANES:]
-        side = pltpu.roll(mixed(2 * q + 1, faces, faces_turned), width, 1)
-        skin = jnp.where(lane < width, mixed(2 * q, faces, faces_turned), jnp.where(left, side, beyond))
-        quarters.append((jnp.where(left, first, second), skin))
+            own = own + jnp.where(left, 0.0, folds[32:, :LANES])
+            moved = jnp.where(left, pltpu.roll(cells[0], half // 2, 1), pltpu.roll(cells[0], half, 1))
+            beyond = 0.25 * moved + folds[:32, LANES:]
+        quarters.append((own, jnp.where(spare, beyond, skin)))
     return quarters
 
 
 def skin_quarters(product):
     half = LANES // 2
     lane = lax.broadcasted_iota(jnp.int32, (32, LANES), 1)
-    face_of = jnp.where(lane < half, (lane // E) % 4, 4)
+    left = lane < half
+    face_of = jnp.where(lane % half < half // 2, (lane // E) % 4, 4)
     sides = [0.25 * product[32 * f : 32 * f + 32, :LANES] for f in range(4)]
     ends = []
     for f in (4, 5):
         end = 0.25 * product[32 * f : 32 * f + 32, LANES:]
-        ends.append(jnp.concatenate([end, end], axis=1))
+        end = jnp.concatenate([end, end], axis=1)
+        ends.append(jnp.where(left, pltpu.roll(end, half // 2, 1), end))
     quarters = []
     for q in range(E // 2):
         value = ends[1] if q == 0 else ends[0] if q == E // 2 - 1 else jnp.zeros_like(sides[0])
         for f in range(4):
-            shift = (E * (f - q) - (half if f >= 2 else 0)) % LANES
+            shift = (E * (f - q) - (half // 2 if f >= 2 else 0)) % LANES
             moved = pltpu.roll(sides[f], shift, 1) if shift else sides[f]
             value = jnp.where(face_of == f, moved, value)
         quarters.append(value)
@@ -577,13 +589,13 @@
         quarter_ref[q, 1] = skin
     for delta in range(4):
         for part in range(3):
-            out_refs[delta][part] = quarter_ref[tile_id ^ delta, part][:channels]
+            out_refs[delta][pl.ds(part, channels, stride=3), :] = quarter_ref[tile_id ^ delta, part][:channels]
 
 
 def fine_kernel(channels, coarse_total, arrived_ref, near_ref, fine_ref, source_ref, turn_ref):
     first = lax.axis_index("brick") * CB_DEV - CB_DEV // 2
     lane = lax.broadcasted_iota(jnp.int32, (8, LANES), 1)
-    group = jnp.where(lane < LANES // 2, (lane // E) % 4, 4)
+    group = jnp.where(lane % (LANES // 2) < 4 * E, (lane // E) % 4, 4)
     x_face = jnp.where(lax.axis_index("tile") < 2, 0, 1)
     for i in range(CB_DEV):
         near = [(near_ref[i, face] - first + coarse_total) % coarse_total for face in (3, 2, 5, 4, x_face)]
@@ -627,9 +639,11 @@
     tile_id = lax.axis_index("tile")
     for delta, ref in enumerate((zero_ref, one_ref, two_ref, three_ref)):
         hold_ref[tile_id ^ delta] = ref[...]
-    skins = [hold_ref[2, 2], hold_ref[3, 2]]
-    skins += [hold_ref[j, 1] for j in range(4)]
-    skins += [hold_ref[0, 2], hold_ref[1, 2]]
+
+    def part(tile, which):
+        return hold_ref[tile, pl.ds(which, channels, stride=3), :]
+
+    skins = [part(2, 2), part(3, 2)] + [part(j, 1) for j in range(4)] + [part(0, 2), part(1, 2)]
     gathered = []
     for i in range(4):
         source = jnp.broadcast_to(source_ref[i, :1], (channels, LANES))
@@ -644,7 +658,7 @@
         moved = jnp.dot(high_part, table, preferred_element_type=jnp.float32) + jnp.dot(
             low_part, table, preferred_element_type=jnp.float32
         )
-        out_ref[pl.ds(i, channels, stride=4), :] = hold_ref[i, 0] + moved
+        out_ref[pl.ds(i, channels, stride=4), :] = part(i, 0) + moved
 
 
 def family_body(sample_grad, sample_brick, sample_slot, neighbour):
@@ -682,7 +696,7 @@
         name="pack",
     )(*[pltpu.with_memory_space_constraint(value, pltpu.HBM) for value in inputs])
     arrived = lax.all_to_all(packed, ("brick", "tile"), 0, 0, tiled=True)
-    message = jax.ShapeDtypeStruct((3, channels, LANES), jnp.float32)
+    message = jax.ShapeDtypeStruct((3 * channels, LANES), jnp.float32)
     messages = pl.pallas_call(
         functools.partial(coarse_kernel, channels),
         out_shape=(message,) * 4,
@@ -717,7 +731,7 @@
         out_shape=jax.ShapeDtypeStruct((channels * CB_DEV, LANES), jnp.float32),
         in_specs=[vmem] * 6,
         out_specs=vmem,
-        scratch_shapes=[pltpu.VMEM((4, 3, channels, LANES), jnp.float32)],
+        scratch_shapes=[pltpu.VMEM((4, 3 * channels, LANES), jnp.float32)],
         compiler_params=limit,
         name="combine",
     )(source, messages[0], arrivals[1], arrivals[2], arrivals[3], jnp.asarray(expand_tables(E), jnp.bfloat16))

time: 29.8 us -> 29.6 us (level)
  no operation moved by 1% of the time
where the time goes in v6:
time: 29.6 us; the launch traced here: 29.4 us
  blocking collectives  17.4 us (59%)
  Pallas kernels  5.49 us (19%)
  starting transfers between devices  4.45 us (15%)
  waiting for transfers between devices  1.45 us (5%)
  between operations  0.66 us (2%)
    all_to_all x1, blocking collectives, family_body(): arrived = lax.all_to_all(packed, ('brick', 'tile'), 0, 0, tiled=True)  17.4 us
    ppermute x3, starting transfers between devices, family_body(): lax.ppermute(messages[delta], 'tile', [(t, t ^ delta) for t in range(tile...  4.45 us
    pallas_call x1, Pallas kernels, family_body(): pl.pallas_call(functools.partial(fine_kernel, channels, CB_DEV * owners),...  2.25 us
    ppermute x3, waiting for transfers between devices, family_body(): lax.ppermute(messages[delta], 'tile', [(t, t ^ delta) for t in range(tile...  1.45 us
    pallas_call x1, Pallas kernels, family_body(): pl.pallas_call(functools.partial(pack_kernel, group_len, tile_count, tupl...  1.36 us
    pallas_call x1, Pallas kernels, family_body(): pl.pallas_call(functools.partial(coarse_kernel, channels), out_shape=(mes...  1.05 us
    pallas_call x1, Pallas kernels, family_body(): pl.pallas_call(functools.partial(combine_kernel, channels), out_shape=jax...  0.82 us
  transfers between devices with their start and end apart: 3, of which 2 were waited for; matrix products, arithmetic and copies ran while one was open for 0% of the time, Pallas kernels for 8%

profile of v6, /device:TPU:0, one launch (start us, length us, event | category | flops | bytes accessed | tf_op | source)
XLA Modules:
  0.0 29.4 jit_solution(13893032505686261999)
XLA Ops:
  0.6 1.4 %pack.1 = bf16[32,2,16,128]{3,2,1,0:T(8,128)(2,1)S(1)} custom-call(s32[8,128]{1,0:T(8,128)} %bitcast.9, s32[8,128]{1,0:T(8,128)} %bitcast.10, bf16[28,1024]{1,0:T(8,128)(2,1)} %grad_hbm.1), custom_call_target="tpu_custom_call" | custom-call | tf_op jit(solution)/shard_map/pack/pallas_call | solution.py:683
  2.0 17.4 %all_to_all.5.arrived_ref = bf16[32,2,16,128]{3,2,1,0:T(8,128)(2,1)S(1)} all-to-all(bf16[32,2,16,128]{3,2,1,0:T(8,128)(2,1)S(1)} %pack.1), channel_id=1, replica_groups=mesh['brick'=8,'tile'=4] {'brick','tile'}, dimensions={0} | all-to-all | bytes 524288 | tf_op jit(solution)/shard_map/all_to_all | solution.py:698
  19.4 1.1 %coarse.1 = (f32[84,128]{1,0:T(8,128)S(1)}, f32[84,128]{1,0:T(8,128)S(1)}, f32[84,128]{1,0:T(8,128)S(1)}, f32[84,128]{1,0:T(8,128)S(1)}) custom-call(bf16[32,2,16,128]{3,2,1,0:T(8,128)(2,1)S(1)} %all_to_all.5.arrived_ref, bf16[128,256]{1,0:T(8,128)(2,1)} %constant.4.clone.table_hbm), custom_call_target="tpu_custom_call" | custom-call | tf_op jit(solution)/shard_map/coarse/pallas_call | solution.py:700
  20.4 0.0 copy-start.1
  20.4 0.8 %collective-permute-start = (f32[84,128]{1,0:T(8,128)S(1)}, f32[84,128]{1,0:T(8,128)S(1)}, u32[]{:S(2)}, u32[]{:S(2)}) collective-permute-start(f32[84,128]{1,0:T(8,128)S(1)} %get-tuple-element.11), channel_id=1, source_target_pairs={{0,1},{1,0},{2,3},{3,2},{4,5},{5,4},{6,7},{7,6},{8,9},{9,8},{10,11... | collective-permute-start | bytes 129032 | tf_op jit(solution)/shard_map/ppermute | solution.py:716
  21.2 1.6 %collective-permute-start.1 = (f32[84,128]{1,0:T(8,128)S(1)}, f32[84,128]{1,0:T(8,128)S(1)}, u32[]{:S(2)}, u32[]{:S(2)}) collective-permute-start(f32[84,128]{1,0:T(8,128)S(1)} %get-tuple-element.12), channel_id=1, source_target_pairs={{0,2},{1,3},{2,0},{3,1},{4,6},{5,7},{6,4},{7,5},{8,10},{9,11},{10,... | collective-permute-start | bytes 129032 | tf_op jit(solution)/shard_map/ppermute | solution.py:716
  22.7 0.0 copy-start
  22.8 2.1 %collective-permute-start.2 = (f32[84,128]{1,0:T(8,128)S(1)}, f32[84,128]{1,0:T(8,128)S(1)}, u32[]{:S(2)}, u32[]{:S(2)}) collective-permute-start(f32[84,128]{1,0:T(8,128)S(1)} %get-tuple-element.13), channel_id=1, source_target_pairs={{0,3},{1,2},{2,1},{3,0},{4,7},{5,6},{6,5},{7,4},{8,11},{9,10},{10,... | collective-permute-start | bytes 129032 | tf_op jit(solution)/shard_map/ppermute | solution.py:716
  24.9 0.0 copy-done.1
  24.9 2.3 %fine.1 = (f32[224,512]{1,0:T(8,128)}, s32[4,8,128]{2,1,0:T(8,128)S(1)}) custom-call(bf16[32,2,16,128]{3,2,1,0:T(8,128)(2,1)S(1)} %all_to_all.5.arrived_ref, s32[4,6]{1,0:T(4,128)S(1)} %copy-done.1), custom_call_target="tpu_custom_call" | custom-call | tf_op jit(solution)/shard_map/fine/pallas_call | solution.py:717
  27.1 0.0 collective-permute-done.one_ref
  27.1 0.4 %collective-permute-done.1.two_ref = f32[84,128]{1,0:T(8,128)S(1)} collective-permute-done((f32[84,128]{1,0:T(8,128)S(1)}, f32[84,128]{1,0:T(8,128)S(1)}, u32[]{:S(2)}, u32[]{:S(2)}) %collective-permute-start.1) | collective-permute-done | bytes 43040 | tf_op jit(solution)/shard_map/ppermute | solution.py:716
  27.5 1.1 %collective-permute-done.2.three_ref = f32[84,128]{1,0:T(8,128)S(1)} collective-permute-done((f32[84,128]{1,0:T(8,128)S(1)}, f32[84,128]{1,0:T(8,128)S(1)}, u32[]{:S(2)}, u32[]{:S(2)}) %collective-permute-start.2) | collective-permute-done | bytes 43040 | tf_op jit(solution)/shard_map/ppermute | solution.py:716
  28.6 0.0 copy-done
  28.6 0.8 %combine.1 = f32[112,128]{1,0:T(8,128)} custom-call(s32[4,8,128]{2,1,0:T(8,128)S(1)} %get-tuple-element.9.source_ref, f32[84,128]{1,0:T(8,128)S(1)} %get-tuple-element.10.zero_ref, f32[84,128]{1,0:T(8,128)S(1)} %collective-permute-done.one_ref, f32[84,128]{1,0:T(8,128)S(1)} %collective-permute-done.1.two_ref, ...), custom_call_target="tpu_custom_call" | custom-call | tf_op jit(solution)/shard_map/combine/pallas_call | solution.py:729
Async XLA Ops:
  20.4 4.5 %copy-start.1 = (s32[4,6]{1,0:T(4,128)S(1)}, s32[4,6]{1,0:T(4,128)}, u32[]{:S(2)}) copy-start(s32[4,6]{1,0:T(4,128)} %near_ref.1) | copy-start | bytes 292
  20.4 6.7 %collective-permute-start = (f32[84,128]{1,0:T(8,128)S(1)}, f32[84,128]{1,0:T(8,128)S(1)}, u32[]{:S(2)}, u32[]{:S(2)}) collective-permute-start(f32[84,128]{1,0:T(8,128)S(1)} %get-tuple-element.11), channel_id=1, source_target_pairs={{0,1},{1,0},{2,3},{3,2},{4,5},{5,4},{6,7},{7,6},{8,9},{9,8},{10,11... | collective-permute-start | bytes 129032 | tf_op jit(solution)/shard_map/ppermute | solution.py:716
  21.2 6.4 %collective-permute-start.1 = (f32[84,128]{1,0:T(8,128)S(1)}, f32[84,128]{1,0:T(8,128)S(1)}, u32[]{:S(2)}, u32[]{:S(2)}) collective-permute-start(f32[84,128]{1,0:T(8,128)S(1)} %get-tuple-element.12), channel_id=1, source_target_pairs={{0,2},{1,3},{2,0},{3,1},{4,6},{5,7},{6,4},{7,5},{8,10},{9,11},{10,... | collective-permute-start | bytes 129032 | tf_op jit(solution)/shard_map/ppermute | solution.py:716
  22.7 5.8 %copy-start = (bf16[2,128,128]{2,1,0:T(8,128)(2,1)S(1)}, bf16[2,128,128]{2,1,0:T(8,128)(2,1)}, u32[]{:S(2)}) copy-start(bf16[2,128,128]{2,1,0:T(8,128)(2,1)} %constant.5.clone.table_ref) | copy-start | bytes 196612
  22.8 5.8 %collective-permute-start.2 = (f32[84,128]{1,0:T(8,128)S(1)}, f32[84,128]{1,0:T(8,128)S(1)}, u32[]{:S(2)}, u32[]{:S(2)}) collective-permute-start(f32[84,128]{1,0:T(8,128)S(1)} %get-tuple-element.13), channel_id=1, source_target_pairs={{0,3},{1,2},{2,1},{3,0},{4,7},{5,6},{6,5},{7,4},{8,11},{9,10},{10,... | collective-permute-start | bytes 129032 | tf_op jit(solution)/shard_map/ppermute | solution.py:716
